TPU v7x, 32 devices: a whole 2x2x4 slice. The times are simulated.
32 devices in a mesh: grp: 2 (over x), row: 16 (over z, y, core).
Axes of the slice: x: 2, y: 2, z: 4, core: 2. Of those that a mesh axis runs over, the one named last changes fastest.
Arguments:
- positions: float32 [3, 12288], P(None, ('grp', 'row')), parts along dimension 1, may hold values from -6 to 6
- noise: float32 [3, 12288], P(None, ('grp', 'row')), parts along dimension 1, may hold values from -6 to 6
- atom_single: bfloat16 [12288, 128], P(('grp', 'row')), parts along dimension 0, may hold values from -6 to 6
- atom_token: int32 [12288], P(('grp', 'row')), parts along dimension 0, may hold values from 0 to 511, as said below
- atom_counts: int32 [32], P(('grp', 'row')), parts along dimension 0, may hold values from 192 to 384, as said below
- window_offsets: int32 [384], P(('grp', 'row')), parts along dimension 0, may hold values from -64 to -32
- atom_bias: float32 [4, 12288, 128], P(None, ('grp', 'row')), parts along dimension 1, may hold values from -4 to 302
- token_single: bfloat16 [1024, 768], P(('grp', 'row')), parts along dimension 0, may hold values from -6 to 6
- token_bias: float32 [16, 1024, 512], P(None, ('grp', 'row')), parts along dimension 1, may hold values from -9 to 302
- pair_mask: int32 [1024, 512], P(('grp', 'row')), parts along dimension 0, may hold values from 0 to 1, as said below
- w_coord: float32 [3, 128], replicated, may hold values from -3.5 to 3.5
- w_atom_qkv: bfloat16 [128, 384], replicated, may hold values from -0.5 to 0.5
- w_atom_out: bfloat16 [128, 128], replicated, may hold values from -0.5 to 0.5
- w_agg: bfloat16 [128, 768], replicated, may hold values from -0.5 to 0.5
- w_tok_qkv: bfloat16 [768, 2304], replicated, may hold values from -0.21875 to 0.21875
- w_tok_gate: bfloat16 [768, 768], replicated, may hold values from -0.21875 to 0.21875
- w_tok_out: bfloat16 [768, 768], replicated, may hold values from -0.21875 to 0.21875
- w_back: bfloat16 [768, 128], replicated, may hold values from -0.21875 to 0.21875
- w_pos: bfloat16 [3, 128], replicated, may hold values from -0.5 to 0.5
Outputs:
- denoised: float32 [3, 12288], P(None, ('grp', 'row')), parts along dimension 1
- token_out: bfloat16 [1024, 768], P(('grp', 'row')), parts along dimension 0
There are 2 independent parts, one for each index of `grp`. A program takes and returns all parts, laid end to end along the dimension named above; an argument that names none is the same for every part. Nothing has to cross between parts.
Inputs may be any that keep to these rules, and one draw needn't show every extreme that they name: `atom_token`: slots i * 384 to (i + 1) * 384 - 1 name tokens from i * 32 - 32 // 4 to (i + 1) * 32 + 32 // 4; ids never fall along the slots. `atom_counts`: entry i is the number of live slots at the front of slots i * 384 onward; some entry equals 384. `pair_mask`: each token's own column, and the column of its index xor 1, are 1.
All inputs are finite; a program needn't handle non-finite values.
Results may differ from a plain program's by a relative error of at most 0.0075.
Values may be sent and summed in bfloat16 or wider, within the bound.
No kernel may reach another device: no remote copies, remote signals or barrier semaphores. Data moves between devices by JAX's collectives and lax.ppermute only.
A program may use at most 64 MiB of HBM per device.

v0:
```python
import functools

import jax
import jax.numpy as jnp
from jax import lax
from jax.experimental import pallas as pl
from jax.experimental.pallas import tpu as pltpu
from jax.sharding import PartitionSpec as P

AH = 4
TH = 16
QWIN = 32
KWIN = 128
BEHIND = KWIN // 2
AHEAD = KWIN - QWIN

noise_level = 2.0
input_scale = 1.0 / 5.0**0.5
skip_scale = 1.0 / 5.0
output_scale = 2.0 / 5.0**0.5
masked_score = -1e30

F32 = jnp.float32
BF16 = jnp.bfloat16
NT = (((1,), (1,)), ((), ()))


def dot(a, b):
    return jnp.dot(a, b, preferred_element_type=F32)


def dot_nt(a, b):
    return lax.dot_general(a, b, NT, preferred_element_type=F32)


def normalize(values):
    center = values - jnp.mean(values, axis=-1, keepdims=True)
    spread = jnp.mean(center * center, axis=-1, keepdims=True)
    return center * lax.rsqrt(spread + 1e-05)


def iota(shape, dim):
    return lax.broadcasted_iota(jnp.int32, shape, dim)


VMEM = pl.BlockSpec(memory_space=pltpu.VMEM)
SMEM = pl.BlockSpec(memory_space=pltpu.SMEM)
HBM = pl.BlockSpec(memory_space=pltpu.HBM)


def call(body, outs, specs, scratch=(), flops=10**7, limit=8, out_specs=None):
    moved = sum(o.size * o.dtype.itemsize for o in outs)
    held = [spec is HBM for spec in specs]
    run = pl.pallas_call(
        body,
        out_shape=tuple(outs),
        in_specs=specs,
        out_specs=tuple(out_specs or [VMEM] * len(outs)),
        scratch_shapes=list(scratch),
        cost_estimate=pl.CostEstimate(flops=flops, bytes_accessed=moved, transcendentals=0),
        compiler_params=pltpu.CompilerParams(vmem_limit_bytes=limit * 2**20),
    )
    return lambda *args: run(*[pltpu.with_memory_space_constraint(x, pltpu.HBM) if h and x.size > 1 else x for x, h in zip(args, held)])


def shape(dims, dtype):
    return jax.ShapeDtypeStruct(dims, dtype)


def fetch(sems, *moves):
    copies = [pltpu.make_async_copy(src, dst, sems.at[n]) for n, (src, dst) in enumerate(moves)]
    for copy in copies:
        copy.start()
    return copies


def quarters(src, dst):
    step = src.shape[0] // 4
    return [(src.at[pl.ds(n * step, step)], dst.at[pl.ds(n * step, step)]) for n in range(4)]


def embed_body(
    counts_hbm,
    pos_hbm,
    noise_hbm,
    single_hbm,
    wc_hbm,
    wqkv_hbm,
    offsets_hbm,
    token_hbm,
    bias_hbm,
    wout_hbm,
    wagg_hbm,
    info_ref,
    start_ref,
    normed_ref,
    pair_ref,
    odd_ref,
    offsets_ref,
    token_ref,
    bias_ref,
    wout_ref,
    wagg_ref,
    wqkv_ref,
    counts_ref,
    pos_ref,
    noise_ref,
    single_ref,
    wc_ref,
    wide_ref,
    sems,
):
    copies = fetch(
        sems,
        (pos_hbm, pos_ref),
        (noise_hbm, noise_ref),
        (wc_hbm, wc_ref),
        (single_hbm, single_ref),
        (counts_hbm, counts_ref),
        (wqkv_hbm, wqkv_ref),
        (offsets_hbm, offsets_ref),
        (token_hbm, token_ref.at[0]),
        *quarters(bias_hbm, bias_ref),
        (wout_hbm, wout_ref),
        (wagg_hbm, wagg_ref),
    )
    rows, width = single_ref.shape
    wide_ref[rows:, :] = jnp.zeros((AHEAD, width), F32)
    for copy in copies[:3]:
        copy.wait()
    scaled = input_scale * (pos_ref[...] + noise_level * noise_ref[...])
    padded = jnp.concatenate([scaled, jnp.zeros((5, rows), F32)], axis=0)
    across = jnp.transpose(padded)
    copies[3].wait()
    start = single_ref[...].astype(F32)
    for c in range(3):
        start = start + across[:, c : c + 1] * wc_ref[c : c + 1, :]
    start_ref[...] = start
    normed = normalize(start)
    normed_ref[...] = normed.astype(BF16)
    wide_ref[:rows, :] = normed
    copies[4].wait()
    live = counts_ref[0, 0]
    me = lax.axis_index("row")
    info_ref[0] = live
    info_ref[1] = me
    info_ref[2] = lax.axis_size("row") - 1
    tail = live - BEHIND
    even = me % 2 == 0
    pair_ref[...] = wide_ref[pl.ds(jnp.where(even, tail, 0), AHEAD), :].astype(BF16)
    odd_ref[...] = wide_ref[pl.ds(jnp.where(even, 0, tail), AHEAD), :].astype(BF16)
    for copy in copies[5:]:
        copy.wait()


def windows_of(queries, keys, values, biases, masks):
    width = queries[0].shape[1]
    depth = width // AH
    rows = AH * QWIN
    own_head = iota((rows, width), 0) // QWIN == iota((rows, width), 1) // depth
    lane_head = iota((QWIN, width), 1) // depth
    stacked = [jnp.where(own_head, jnp.concatenate([q] * AH, axis=0), 0.0).astype(BF16) for q in queries]
    scores = [dot_nt(q, k) * (1.0 / depth**0.5) + b for q, k, b in zip(stacked, keys, biases)]
    if masks is not None:
        scores = [jnp.where(m, s, masked_score) for m, s in zip(masks, scores)]
    tops = [jnp.max(s, axis=-1, keepdims=True) for s in scores]
    scores = [jnp.exp(s - t) for s, t in zip(scores, tops)]
    shares = [1.0 / jnp.sum(s, axis=-1, keepdims=True) for s in scores]
    weights = [(s * r).astype(BF16) for s, r in zip(scores, shares)]
    mixed = [dot(w, v) for w, v in zip(weights, values)]
    outs = []
    for mix in mixed:
        out = mix[:QWIN]
        for h in range(1, AH):
            out = jnp.where(lane_head == h, mix[h * QWIN : (h + 1) * QWIN], out)
        outs.append(out.astype(BF16))
    return outs


def local_body(offsets, normed_ref, wqkv_ref, bias_ref, q_ref, k_ref, v_ref, att_ref):
    rows, width = normed_ref.shape
    qkv = dot(normed_ref[...], wqkv_ref[...]).astype(BF16)
    q_ref[...] = qkv[:, :width]
    for n, ref in enumerate((k_ref, v_ref)):
        ref[:rows, :] = qkv[:, (n + 1) * width : (n + 2) * width].astype(F32)
        ref[rows:, :] = jnp.zeros((AHEAD, width), F32)
    windows = rows // QWIN
    skip = BEHIND // QWIN
    stop = windows - (AHEAD - QWIN) // QWIN
    for part in (slice(0, skip * QWIN), slice(stop * QWIN, rows)):
        att_ref[part, :] = jnp.zeros((part.stop - part.start, width), BF16)
    at = [slice(m * QWIN, (m + 1) * QWIN) for m in range(skip, stop)]
    base = [m * QWIN + offsets[0, m] for m in range(skip, stop)]
    outs = windows_of(
        [q_ref[a, :].astype(F32) for a in at],
        [k_ref[pl.ds(b, KWIN), :].astype(BF16) for b in base],
        [v_ref[pl.ds(b, KWIN), :].astype(BF16) for b in base],
        [bias_ref[:, a, :].reshape(AH * QWIN, KWIN) for a in at],
        None,
    )
    for a, out in zip(at, outs):
        att_ref[a, :] = out


def atoms_body(
    half,
    info,
    offsets,
    token_ref,
    start_ref,
    q_ref,
    k_ref,
    v_ref,
    pair_ref,
    odd_ref,
    att_ref,
    bias_ref,
    wout_ref,
    wagg_ref,
    wqkv_ref,
    mid_ref,
    own_ref,
    pair_out,
    odd_out,
    hot_ref,
    living_ref,
    k_ext,
    v_ext,
    att,
):
    rows, width = start_ref.shape
    live, me, last = info[0], info[1], info[2]
    even = me % 2 == 0
    pair = dot(pair_ref[...], wqkv_ref[:, width:]).astype(BF16).astype(F32)
    odd = dot(odd_ref[...], wqkv_ref[:, width:]).astype(BF16).astype(F32)
    for n, (ref, ext) in enumerate(((k_ref, k_ext), (v_ref, v_ext))):
        at = slice(n * width, (n + 1) * width)
        ext[:BEHIND, :] = jnp.where(even, odd[:BEHIND, at], pair[:BEHIND, at])
        ext[BEHIND : BEHIND + rows + AHEAD, :] = ref[...]
        ext[pl.ds(BEHIND + live, AHEAD), :] = jnp.where(even, pair[:, at], odd[:, at])
    low = jnp.where(me > 0, 0, BEHIND)
    high = BEHIND + live + jnp.where(me < last, AHEAD, 0)
    att[...] = att_ref[...]
    windows = rows // QWIN
    tails = AHEAD // QWIN
    first = jnp.minimum((live - BEHIND) // QWIN, windows - tails)
    chosen = list(range(BEHIND // QWIN)) + [first + n for n in range(tails)]
    at = [pl.ds(pl.multiple_of(m * QWIN, QWIN), QWIN) for m in chosen]
    base = [BEHIND + QWIN * m + offsets[0, m] for m in chosen]
    slots = [b + iota((1, KWIN), 1) for b in base]
    outs = windows_of(
        [q_ref[a, :].astype(F32) for a in at],
        [k_ext[pl.ds(b, KWIN), :].astype(BF16) for b in base],
        [v_ext[pl.ds(b, KWIN), :].astype(BF16) for b in base],
        [bias_ref[:, a, :].reshape(AH * QWIN, KWIN) for a in at],
        [(s >= low) & (s < high) for s in slots],
    )
    for a, out in zip(at, outs):
        att[a, :] = out
    mid = start_ref[...] + dot(att[...], wout_ref[...])
    mid_ref[...] = mid
    spread = jnp.maximum(dot(mid.astype(BF16), wagg_ref[...]), 0.0).astype(BF16)
    block_rows = own_ref.shape[0]
    living = iota((1, rows), 1) < live
    living_ref[...] = living.astype(F32)
    relative = token_ref[...] - (me * block_rows - half)
    hot = ((iota((block_rows + 2 * half, rows), 0) == relative) & living).astype(F32)
    hot_ref[...] = jnp.transpose(hot).astype(BF16)
    sums = dot(hot.astype(BF16), spread)
    counts = jnp.sum(hot, axis=1, keepdims=True)
    first = jnp.minimum(counts, 256.0)
    lane = iota((counts.shape[0], 128), 1)
    packed = jnp.where(lane == 0, first, jnp.where(lane == 1, counts - first, 0.0))
    model = wagg_ref.shape[1]
    own_ref[:, :model] = sums[half : half + block_rows]
    own_ref[:, model:] = packed[half : half + block_rows]
    lower = jnp.concatenate([sums[:half], packed[:half]], axis=1)
    upper = jnp.concatenate([sums[half + block_rows :], packed[half + block_rows :]], axis=1)
    pair_out[...] = jnp.where(even, upper, lower).astype(BF16)
    odd_out[...] = jnp.where(even, lower, upper).astype(BF16)


def token_body(own_ref, pair_ref, odd_ref, single_ref, in_ref, norm_ref):
    me = lax.axis_index("row")
    even = me % 2 == 0
    model = single_ref.shape[1]
    pair = pair_ref[...].astype(F32)
    odd = odd_ref[...].astype(F32)
    lower = jnp.where(me > 0, jnp.where(even, odd, pair), 0.0)
    upper = jnp.where(me < lax.axis_size("row") - 1, jnp.where(even, pair, odd), 0.0)
    both = own_ref[...] + jnp.concatenate([lower, upper], axis=0)
    count = both[:, model : model + 1] + both[:, model + 1 : model + 2]
    token_in = single_ref[...].astype(F32) + both[:, :model] / jnp.maximum(count, 1.0)
    in_ref[...] = token_in
    norm_ref[...] = normalize(token_in).astype(BF16)


def bias_body(after, bias_hbm, mask_hbm, bias_ref, mask_ref, sems):
    for copy in fetch(sems, (mask_hbm, mask_ref), *quarters(bias_hbm, bias_ref)):
        copy.wait()


def query_body(norm_ref, wqkv_ref, query_ref):
    rows, model = norm_ref.shape
    width = model // TH
    group = TH // 2
    span = group * width
    own = iota((group * rows, span), 0) // rows == iota((group * rows, span), 1) // width
    tq = dot(norm_ref[...], wqkv_ref[:, :model])
    for g in range(2):
        part = tq[:, g * span : (g + 1) * span]
        stacked = jnp.where(own, jnp.concatenate([part] * group, axis=0), 0.0).astype(BF16)
        wk = wqkv_ref[:, model + g * span : model + (g + 1) * span]
        query_ref[g * group * rows : (g + 1) * group * rows, :] = dot_nt(stacked, wk).astype(BF16)


def stage_body(lists, after, norm_ref, bias_ref, mask_ref, wgate_hbm, out_ref, gate_ref, wgate_ref, sems):
    copies = fetch(sems, *quarters(wgate_hbm, wgate_ref))

    @pl.when(lax.axis_index("row") >= 0)
    def _():
        heads, rows, _ = bias_ref.shape
        if lists is None:
            allowed = mask_ref[...] == 1
            for h in range(heads):
                out_ref[0, h * rows : (h + 1) * rows, :] = jnp.where(allowed, bias_ref[h], masked_score)
        else:
            me = lax.axis_index("row")
            kind = kind_of(me)
            per = 128 // rows
            lane_block = iota((heads * rows, 128), 1) // rows
            for c in range(len(lists[0])):
                for tile in range(len(lists[0][c]) // per):
                    for j in range(per):
                        n = tile * per + j
                        block = me ^ jnp.where(kind == 0, lists[0][c][n], lists[1][c][n])
                        source = pl.ds(pl.multiple_of((block // per) * 128, 128), 128)
                        piece = jnp.where((mask_ref[:, source] == 1)[None], bias_ref[:, :, source], masked_score)
                        piece = piece.reshape(heads * rows, 128)
                        piece = pltpu.roll(piece, ((j + per - block % per) % per) * rows, 1)
                        merged = piece if j == 0 else jnp.where(lane_block == j, piece, merged)
                    out_ref[c, :, tile * 128 : (tile + 1) * 128] = merged

    for copy in copies:
        copy.wait()
    gate_ref[...] = jax.nn.sigmoid(dot(norm_ref[...], wgate_ref[...]))


def weights_of(copies, in_ref, wout_ref, wback_ref, both_ref, base_ref):
    for copy in copies:
        copy.wait()
    both_ref[...] = dot(wout_ref[...], wback_ref[...]).astype(BF16)
    base_ref[...] = dot(in_ref[...].astype(BF16), wback_ref[...])


def weights_body(in_ref, wout_hbm, wback_hbm, wout_ref, both_ref, base_ref, wback_ref, sems):
    copies = fetch(sems, (wback_hbm, wback_ref), *quarters(wout_hbm, wout_ref))
    weights_of(copies, in_ref, wout_ref, wback_ref, both_ref, base_ref)


def part_of(rows, query_ref, keys_ref, bias, wqkv_ref):
    model = query_ref.shape[1]
    width = model // TH
    group = TH // 2
    span = group * width
    keys = keys_ref[...]
    values = dot(keys, wqkv_ref[:, 2 * model :]).astype(BF16)
    lane_head = iota((rows, span), 1) // width

    def by_head(stacked):
        out = jnp.broadcast_to(stacked[:rows], (rows, span))
        for h in range(1, group):
            out = jnp.where(lane_head == h, stacked[h * rows : (h + 1) * rows], out)
        return out

    found = []
    for g in range(2):
        at = slice(g * group * rows, (g + 1) * group * rows)
        scores = dot_nt(query_ref[at, :], keys) * (1.0 / width**0.5) + bias(at)
        top = jnp.max(scores, axis=-1, keepdims=True)
        scores = jnp.exp(scores - top)
        total = jnp.sum(scores, axis=-1, keepdims=True)
        mixed = dot(scores.astype(BF16), values[:, g * span : (g + 1) * span])
        found.append((by_head(top), by_head(total), by_head(mixed)))
    return [jnp.concatenate([found[0][n], found[1][n]], axis=1) for n in range(3)]


def part_body(chunk, query_ref, keys_ref, bias_ref, wqkv_ref, part_ref):
    found = part_of(part_ref.shape[1], query_ref, keys_ref, lambda at: bias_ref[chunk, at, :], wqkv_ref)
    for n in range(3):
        part_ref[n] = found[n]


def second_body(
    chunk,
    query_ref,
    keys_ref,
    bias_ref,
    wqkv_ref,
    in_ref,
    wout_hbm,
    wback_hbm,
    part_ref,
    wout_ref,
    both_ref,
    base_ref,
    wback_ref,
    sems,
):
    copies = fetch(sems, (wback_hbm, wback_ref), *quarters(wout_hbm, wout_ref))

    @pl.when(lax.axis_index("row") >= 0)
    def _():
        part_body(chunk, query_ref, keys_ref, bias_ref, wqkv_ref, part_ref)

    weights_of(copies, in_ref, wout_ref, wback_ref, both_ref, base_ref)


def attend_body(
    half,
    chunk,
    base_ref,
    query_ref,
    gate_ref,
    keys_ref,
    bias_ref,
    wqkv_ref,
    both_ref,
    *rest,
):
    parts, (gated_ref, back_ref, pair_out, odd_out) = rest[:-4], rest[-4:]
    rows, _ = gate_ref.shape
    even = lax.axis_index("row") % 2 == 0
    found = part_of(rows, query_ref, keys_ref, lambda at: bias_ref[chunk, at, :], wqkv_ref)
    found = [[part[n] for n in range(3)] for part in parts] + [found]
    top = functools.reduce(jnp.maximum, [f[0] for f in found])
    shares = [jnp.exp(f[0] - top) for f in found]
    total = sum(f[1] * w for f, w in zip(found, shares))
    mixed = sum(f[2] * w for f, w in zip(found, shares))
    gated = (gate_ref[...] * (mixed / total)).astype(BF16)
    gated_ref[...] = gated
    back = base_ref[...] + dot(gated, both_ref[...])
    back_ref[...] = back.astype(BF16)
    lower, upper = back[:half], back[rows - half :]
    pair_out[...] = jnp.where(even, upper, lower).astype(BF16)
    odd_out[...] = jnp.where(even, lower, upper).astype(BF16)


def out_body(in_ref, gated_ref, wout_ref, out_ref):
    out_ref[...] = (in_ref[...] + dot(gated_ref[...], wout_ref[...])).astype(BF16)


def final_body(living_ref, hot_ref, mid_ref, back_ref, pair_ref, odd_ref, wpos_ref, pos_ref, noise_ref, out_ref):
    even = lax.axis_index("row") % 2 == 0
    pair = pair_ref[...].astype(F32)
    odd = odd_ref[...].astype(F32)
    near = jnp.concatenate(
        [jnp.where(even, odd, pair), back_ref[...].astype(F32), jnp.where(even, pair, odd)], axis=0
    ).astype(BF16)
    last = mid_ref[...] + dot(hot_ref[...], near)
    update = dot_nt(wpos_ref[...], normalize(last).astype(BF16))
    noisy = pos_ref[...] + noise_level * noise_ref[...]
    out_ref[...] = jnp.where(living_ref[...] > 0.0, skip_scale * noisy + output_scale * update, 0.0)


def exchange(pair, odd, groups, count):
    near = [(i, i ^ 1) for i in range(count) if i ^ 1 < count]
    odds = [(i, i + 1) for i in range(1, count - 1, 2)]
    far = [(g * count + a, g * count + b) for g in range(groups) for a, b in odds + [(b, a) for a, b in odds]]
    if groups % 2 == 0 and count % 2 == 0:
        far += [(g * count + i, (g ^ 1) * count + i) for g in range(groups) for i in (0, count - 1)]
    odd = lax.ppermute(odd, ("grp", "row"), far)
    pair = lax.ppermute(pair, "row", near)
    return pair, odd


def kind_of(i):
    return (i ^ (i >> 1) ^ (i >> 2)) & 1


def gather_plan(count):
    bits = [1 << b for b in range(count.bit_length() - 1, 0, -1) if 1 << b < count]
    steps = [[b | 1, b | 1] for b in bits]
    high, low = bits[-2] | 1, bits[-1] | 1
    steps[-2:] = [[high, low], [low, high]]
    lists = [[0], [0]]
    for step in steps[:-1]:
        lists = [lists[p] + [x ^ step[p] for x in lists[p ^ kind_of(step[p])]] for p in range(2)]
    near = [[1 ^ x for x in lists[1 - p]] for p in range(2)]
    last = [[x ^ steps[-1][p] for x in lists[p]] for p in range(2)]
    end = [[1 ^ x for x in last[1 - p]] for p in range(2)]
    return steps, [[lists[p], near[p], last[p], end[p]] for p in range(2)]


def swap(value, count, step):
    return lax.ppermute(value, "row", [(i, i ^ step[kind_of(i)]) for i in range(count)])


def on_device(
    groups,
    count,
    positions,
    noise,
    atom_single,
    atom_token,
    atom_counts,
    window_offsets,
    atom_bias,
    token_single,
    token_bias,
    pair_mask,
    w_coord,
    w_atom_qkv,
    w_atom_out,
    w_agg,
    w_tok_qkv,
    w_tok_gate,
    w_tok_out,
    w_back,
    w_pos,
):
    rows, width = atom_single.shape
    block_rows, model = token_single.shape
    half = block_rows // 2
    info_shape = shape((8,), jnp.int32)
    info, start, normed, pair, odd, offsets, tokens, bias, wout, wagg, wqkv = call(
        embed_body,
        [
            info_shape,
            shape((rows, width), F32),
            shape((rows, width), BF16),
            shape((AHEAD, width), BF16),
            shape((AHEAD, width), BF16),
            shape((1, rows // QWIN), jnp.int32),
            shape((1, rows), jnp.int32),
            shape(atom_bias.shape, F32),
            shape(w_atom_out.shape, BF16),
            shape(w_agg.shape, BF16),
            shape(w_atom_qkv.shape, BF16),
        ],
        [HBM] * 11,
        [
            pltpu.SMEM((1, 1), jnp.int32),
            pltpu.VMEM(positions.shape, F32),
            pltpu.VMEM(noise.shape, F32),
            pltpu.VMEM(atom_single.shape, BF16),
            pltpu.VMEM(w_coord.shape, F32),
            pltpu.VMEM((rows + AHEAD, width), F32),
            pltpu.SemaphoreType.DMA((14,)),
        ],
        out_specs=[SMEM] + [VMEM] * 4 + [SMEM] + [VMEM] * 5,
    )(
        atom_counts[None],
        positions,
        noise,
        atom_single,
        w_coord,
        w_atom_qkv,
        window_offsets[None],
        atom_token,
        atom_bias,
        w_atom_out,
        w_agg,
    )
    pair, odd = exchange(pair, odd, groups, count)
    q, keys, values, att = call(
        local_body,
        [
            shape((rows, width), BF16),
            shape((rows + AHEAD, width), F32),
            shape((rows + AHEAD, width), F32),
            shape((rows, width), BF16),
        ],
        [SMEM] + [VMEM] * 3,
        flops=10**9,
    )(offsets, normed, wqkv, bias)
    packed = model + 128
    mid, own, pair, odd, hot, living = call(
        functools.partial(atoms_body, half),
        [
            shape((rows, width), F32),
            shape((block_rows, packed), F32),
            shape((half, packed), BF16),
            shape((half, packed), BF16),
            shape((rows, block_rows + 2 * half), BF16),
            shape((1, rows), F32),
        ],
        [SMEM, SMEM] + [VMEM] * 12,
        [pltpu.VMEM((BEHIND + rows + AHEAD, width), F32)] * 2 + [pltpu.VMEM((rows, width), BF16)],
    )(info, offsets, tokens, start, q, keys, values, pair, odd, att, bias, wout, wagg, wqkv)
    pair, odd = exchange(pair, odd, groups, count)
    raw, mask = call(
        bias_body,
        [shape(token_bias.shape, F32), shape(pair_mask.shape, jnp.int32)],
        [VMEM, HBM, HBM],
        [pltpu.SemaphoreType.DMA((5,))],
        flops=10**9,
    )(own, token_bias, pair_mask)
    odd, raw, mask = lax.optimization_barrier((odd, raw, mask))
    token_in, norm = call(
        token_body, [shape((block_rows, model), F32), shape((block_rows, model), BF16)], [VMEM] * 4
    )(own, pair, odd, token_single)

    doubling = count & (count - 1) == 0 and count >= 16 and 128 % block_rows == 0
    steps, lists = gather_plan(count) if doubling else ([], None)
    chunks = 4 if doubling else 1
    span = count * block_rows // chunks

    def query(seen):
        return call(
            query_body, [shape((TH * block_rows, model), BF16)], [VMEM] * 2, flops=10**9
        )(seen, w_tok_qkv)[0]

    def stage(seen):
        return call(
            functools.partial(stage_body, lists),
            [shape((chunks, TH * block_rows, span), F32), shape((block_rows, model), F32)],
            [VMEM] * 4 + [HBM],
            [pltpu.VMEM(w_tok_gate.shape, BF16), pltpu.SemaphoreType.DMA((4,))],
            flops=10**9,
        )(seen, norm, raw, mask, w_tok_gate)

    made = [shape(w_tok_out.shape, BF16), shape(w_back.shape, BF16), shape((block_rows, width), F32)]
    kept = [pltpu.VMEM(w_back.shape, BF16), pltpu.SemaphoreType.DMA((5,))]

    def second(chunk, seen):
        return call(
            functools.partial(second_body, chunk),
            [shape((3, block_rows, model), F32)] + made,
            [VMEM] * 5 + [HBM] * 2,
            kept,
            flops=10**9,
        )(query_rows, seen, score_bias, w_tok_qkv, token_in, w_tok_out, w_back)

    def part(chunk, seen):
        return call(
            functools.partial(part_body, chunk),
            [shape((3, block_rows, model), F32)],
            [VMEM] * 4,
            flops=10**9,
        )(query_rows, seen, score_bias, w_tok_qkv)[0]

    if doubling:
        held = norm
        for n, step in enumerate(steps[:-1]):
            arrived = swap(held, count, step)
            if n == 0:
                arrived, query_rows = lax.optimization_barrier((arrived, query(norm)))
            if n == 1:
                arrived, (score_bias, gate) = lax.optimization_barrier((arrived, stage(held)))
            held = jnp.concatenate([held, arrived], axis=0)
        last = swap(held, count, steps[-1])
        near = swap(held, count, [1, 1])
        after, wout, both, base = second(1, near)
        parts = [part(0, held), after]
        last, parts, wout, both, base = lax.optimization_barrier((last, parts, wout, both, base))
        end = swap(last, count, [1, 1])
        parts = parts + [part(2, last)]
    else:
        end = lax.all_gather(norm, "row", axis=0, tiled=True)
        query_rows = query(norm)
        score_bias, gate = stage(norm)
        wout, both, base = call(weights_body, made, [VMEM] + [HBM] * 2, kept)(token_in, w_tok_out, w_back)
        parts = []
    gated, back, pair, odd = call(
        functools.partial(attend_body, half, chunks - 1),
        [
            shape((block_rows, model), BF16),
            shape((block_rows, width), BF16),
            shape((half, width), BF16),
            shape((half, width), BF16),
        ],
        [VMEM] * (7 + len(parts)),
    )(base, query_rows, gate, end, score_bias, w_tok_qkv, both, *parts)
    pair, odd = exchange(pair, odd, groups, count)
    (token_out,) = call(
        out_body, [shape((block_rows, model), BF16)], [VMEM] * 3, flops=10**9
    )(token_in, gated, wout)
    odd, token_out = lax.optimization_barrier((odd, token_out))
    (denoised,) = call(
        final_body, [shape(positions.shape, F32)], [VMEM] * 9
    )(living, hot, mid, back, pair, odd, w_pos, positions, noise)
    return (denoised, token_out)


def solution(mesh):
    placed = (
        P(None, ("grp", "row")),
        P(None, ("grp", "row")),
        P(("grp", "row"), None),
        P(("grp", "row")),
        P(("grp", "row")),
        P(("grp", "row")),
        P(None, ("grp", "row"), None),
        P(("grp", "row"), None),
        P(None, ("grp", "row"), None),
        P(("grp", "row"), None),
    ) + (P(),) * 9
    return jax.shard_map(
        functools.partial(on_device, mesh.shape["grp"], mesh.shape["row"]),
        mesh=mesh,
        in_specs=placed,
        out_specs=(P(None, ("grp", "row")), P(("grp", "row"), None)),
        check_vma=False,
    )
```

profile of v0, /device:TPU:24, one launch (start us, length us, event | category | flops | bytes accessed | tf_op | source)
XLA Modules:
  0.0 37.9 jit_solution(15061015048562430732)
XLA Ops:
  1.3 2.1 %shard_map.194 = (s32[8]{0:T(128)S(1)}, f32[384,128]{1,0:T(8,128)S(1)}, bf16[384,128]{1,0:T(8,128)(2,1)S(1)}, bf16[96,128]{1,0:T(8,128)(2,1)S(1)}, bf16[96,128]{...) custom-call(s32[1,1]{1,0:T(1,128)} %bitcast.2.counts_hbm, ...), custom_call_target="tpu_custom_call" | custom-call | flops 10000000 | bytes 1459792 | tf_op jit(solution)/shard_map/pallas_call | solution.py:63
  3.5 1.5 %collective-permute-start.1 = (bf16[96,128]{1,0:T(8,128)(2,1)S(1)}, bf16[96,128]{1,0:T(8,128)(2,1)S(1)}, u32[]{:S(2)}, u32[]{:S(2)}) collective-permute-start(bf16[96,128]{1,0:T(8,128)(2,1)S(1)} %get-tuple-element.64), channel_id=1, source_target_pairs={{1,2},{3,4},{5,6},{7,8},{9,10},{11,12},{13,14},{2,1},{4,3},{6,5},{... | collective-permute-start | bytes 73736 | tf_op jit(solution)/shard_map/ppermute | solution.py:472
  5.0 1.5 %shard_map.195 = (bf16[384,128]{1,0:T(8,128)(2,1)S(1)}, f32[480,128]{1,0:T(8,128)S(1)}, f32[480,128]{1,0:T(8,128)S(1)}, bf16[384,128]{1,0:T(8,128)(2,1)S(1)}) custom-call(s32[1,12]{1,0:T(1,128)S(1)} %get-tuple-element.54.offsets, bf16[384,128]{1,0:T(8,128)(2,1)S(1)} %get-tuple-element.57.normed_ref, bf16[128,384]{1,0:T(8,128)(2,1)S(1)} %get-tuple-element.58.wqkv_ref, ...), custom_call_target="tpu_custom_call" | custom-call | flops 1000000000 | bytes 688128 | tf_op jit(solution)/shard_map/pallas_call | solution.py:63
  6.5 1.2 %collective-permute-done.1.odd_ref = bf16[96,128]{1,0:T(8,128)(2,1)S(1)} collective-permute-done((bf16[96,128]{1,0:T(8,128)(2,1)S(1)}, bf16[96,128]{1,0:T(8,128)(2,1)S(1)}, u32[]{:S(2)}, u32[]{:S(2)}) %collective-permute-start.1) | collective-permute-done | bytes 24608 | tf_op jit(solution)/shard_map/ppermute | solution.py:472
  7.7 1.8 %shard_map.196 = (f32[384,128]{1,0:T(8,128)S(1)}, f32[32,896]{1,0:T(8,128)S(1)}, bf16[16,896]{1,0:T(8,128)(2,1)S(1)}, bf16[16,896]{1,0:T(8,128)(2,1)S(1)}, bf16[...) custom-call(s32[8]{0:T(128)S(1)} %get-tuple-element.53.info, s32[1,12]{1,0:T(1,128)S(1)} %get-tuple-element.54.offsets, ...), custom_call_target="tpu_custom_call" | custom-call | flops 10000000 | bytes 419328 | tf_op jit(solution)/shard_map/pallas_call | solution.py:63
  9.7 1.5 %collective-permute-start.3 = (bf16[16,896]{1,0:T(8,128)(2,1)S(1)}, bf16[16,896]{1,0:T(8,128)(2,1)S(1)}, u32[]{:S(2)}, u32[]{:S(2)}) collective-permute-start(bf16[16,896]{1,0:T(8,128)(2,1)S(1)} %get-tuple-element.73), channel_id=1, source_target_pairs={{1,2},{3,4},{5,6},{7,8},{9,10},{11,12},{13,14},{2,1},{4,3},{6,5},{... | collective-permute-start | bytes 86024 | tf_op jit(solution)/shard_map/ppermute | solution.py:472
  11.2 1.4 %shard_map.197 = (f32[16,32,512]{2,1,0:T(8,128)S(1)}, s32[32,512]{1,0:T(8,128)S(1)}) custom-call(f32[32,896]{1,0:T(8,128)S(1)} %get-tuple-element.71.after.own_ref, f32[16,32,512]{2,1,0:T(8,128)} %bias_hbm.3, s32[32,512]{1,0:T(8,128)} %mask_hbm.1), custom_call_target="tpu_custom_call" | custom-call | flops 1000000000 | bytes 1114112 | tf_op jit(solution)/shard_map/pallas_call | solution.py:63
  12.6 1.4 %collective-permute-done.3.odd_ref = bf16[16,896]{1,0:T(8,128)(2,1)S(1)} collective-permute-done((bf16[16,896]{1,0:T(8,128)(2,1)S(1)}, bf16[16,896]{1,0:T(8,128)(2,1)S(1)}, u32[]{:S(2)}, u32[]{:S(2)}) %collective-permute-start.3) | collective-permute-done | bytes 28704 | tf_op jit(solution)/shard_map/ppermute | solution.py:472
  13.9 0.3 shard_map.198
  14.4 0.8 %shard_map.199.query_ref = bf16[512,768]{1,0:T(8,128)(2,1)S(1)} custom-call(bf16[32,768]{1,0:T(8,128)(2,1)S(1)} %get-tuple-element.77.norm_ref, bf16[768,2304]{1,0:T(8,128)(2,1)S(1)} %copy-done), custom_call_target="tpu_custom_call" | custom-call | flops 1000000000 | bytes 786432 | tf_op jit(solution)/shard_map/pallas_call | solution.py:63
  15.2 5.0 %collective-permute-done.4 = bf16[32,768]{1,0:T(8,128)(2,1)S(1)} collective-permute-done((bf16[32,768]{1,0:T(8,128)(2,1)S(1)}, bf16[32,768]{1,0:T(8,128)(2,1)S(1)}, u32[]{:S(2)}, u32[]{:S(2)}) %collective-permute-start.4) | collective-permute-done | bytes 49184 | tf_op jit(solution)/shard_map/ppermute | solution.py:496
  20.3 1.6 %shard_map.200 = (f32[4,512,128]{2,1,0:T(8,128)S(1)}, f32[32,768]{1,0:T(8,128)S(1)}) custom-call(bf16[64,768]{1,0:T(8,128)(2,1)S(1)} %get-tuple-element.104.after, bf16[32,768]{1,0:T(8,128)(2,1)S(1)} %get-tuple-element.77.norm_ref, f32[16,32,512]{2,1,0:T(8,128)S(1)} %get-tuple-element.79.bias_ref, s32[32,512]{1,0:T(8,128)S(1)} %get-tuple-element.80.mask_ref, ...), custom_call_target="tpu_custom_call" | custom-call | flops 1000000000 | bytes 1146880 | tf_op jit(solution)/shard_map/pallas_call | solution.py:63
  21.9 2.4 %collective-permute-done.5 = bf16[64,768]{1,0:T(8,128)(2,1)S(1)} collective-permute-done((bf16[64,768]{1,0:T(8,128)(2,1)S(1)}, bf16[64,768]{1,0:T(8,128)(2,1)S(1)}, u32[]{:S(2)}, u32[]{:S(2)}) %collective-permute-start.5) | collective-permute-done | bytes 98336 | tf_op jit(solution)/shard_map/ppermute | solution.py:496
  24.5 1.1 %shard_map.201.rest_0_ = f32[3,32,768]{2,1,0:T(8,128)S(1)} custom-call(bf16[512,768]{1,0:T(8,128)(2,1)S(1)} %shard_map.199.query_ref, bf16[128,768]{1,0:T(8,128)(2,1)S(1)} %constant_dynamic-update-slice_fusion.2.keys_ref, f32[4,512,128]{2,1,0:T(8,128)S(1)} %get-tuple-element.85.bias_ref, bf16[768,2304]{1,0:T(8,128)(2,1)S(1)} %copy-done), custom_call_target="tpu_custom_call" | custom-call | flops 1000000000 | bytes 294912 | tf_op jit(solution)/shard_map/pallas_call | solution.py:63
  25.7 0.2 collective-permute-done.7.keys_ref
  25.9 1.9 %shard_map.202 = (f32[3,32,768]{2,1,0:T(8,128)S(1)}, bf16[768,768]{1,0:T(8,128)(2,1)S(1)}, bf16[768,128]{1,0:T(8,128)(2,1)S(1)}, f32[32,128]{1,0:T(8,128)S(1)}) custom-call(bf16[512,768]{1,0:T(8,128)(2,1)S(1)} %shard_map.199.query_ref, bf16[128,768]{1,0:T(8,128)(2,1)S(1)} %collective-permute-done.7.keys_ref, f32[4,512,128]{2,1,0:T(8,128)S(1)} %get-tuple-element.85.bias_ref, ...), custom_call_target="tpu_custom_call" | custom-call | flops 1000000000 | bytes 1687552 | tf_op jit(solution)/shard_map/pallas_call | solution.py:63
  27.8 1.9 %collective-permute-done.6.keys_ref = bf16[128,768]{1,0:T(8,128)(2,1)S(1)} collective-permute-done((bf16[128,768]{1,0:T(8,128)(2,1)S(1)}, bf16[128,768]{1,0:T(8,128)(2,1)S(1)}, u32[]{:S(2)}, u32[]{:S(2)}) %collective-permute-start.6) | collective-permute-done | bytes 196640 | tf_op jit(solution)/shard_map/ppermute | solution.py:496
  29.6 0.4 %collective-permute-start.8 = (bf16[128,768]{1,0:T(8,128)(2,1)S(1)}, bf16[128,768]{1,0:T(8,128)(2,1)S(1)}, u32[]{:S(2)}, u32[]{:S(2)}) collective-permute-start(bf16[128,768]{1,0:T(8,128)(2,1)S(1)} %collective-permute-done.6.keys_ref), channel_id=1, source_target_pairs={{0,1},{1,0},{2,3},{3,2},{4,5},{5,4},{6,7},{7,6},{8,9},{9,8},{10,11... | collective-permute-start | bytes 589832 | tf_op jit(solution)/shard_map/ppermute | solution.py:496
  30.0 1.1 %shard_map.203.rest_2_ = f32[3,32,768]{2,1,0:T(8,128)S(1)} custom-call(bf16[512,768]{1,0:T(8,128)(2,1)S(1)} %shard_map.199.query_ref, bf16[128,768]{1,0:T(8,128)(2,1)S(1)} %collective-permute-done.6.keys_ref, f32[4,512,128]{2,1,0:T(8,128)S(1)} %get-tuple-element.85.bias_ref, bf16[768,2304]{1,0:T(8,128)(2,1)S(1)} %copy-done), custom_call_target="tpu_custom_call" | custom-call | flops 1000000000 | bytes 294912 | tf_op jit(solution)/shard_map/pallas_call | solution.py:63
  31.2 1.3 %shard_map.204 = (bf16[32,768]{1,0:T(8,128)(2,1)S(1)}, bf16[32,128]{1,0:T(8,128)(2,1)S(1)}, bf16[16,128]{1,0:T(8,128)(2,1)S(1)}, bf16[16,128]{1,0:T(8,128)(2,1)S(1)}) custom-call(f32[32,128]{1,0:T(8,128)S(1)} %get-tuple-element.91.base_ref, bf16[512,768]{1,0:T(8,128)(2,1)S(1)} %shard_map.199.query_ref, f32[32,768]{1,0:T(8,128)S(1)} %get-tuple-element.92.gate_ref, ...), custom_call_target="tpu_custom_call" | custom-call | flops 10000000 | bytes 65536 | tf_op jit(solution)/shard_map/pallas_call | solution.py:63
  32.5 0.3 collective-permute-start.9
  32.9 1.0 %shard_map.205 = bf16[32,768]{1,0:T(8,128)(2,1)} custom-call(f32[32,768]{1,0:T(8,128)S(1)} %get-tuple-element.86.in_ref, bf16[32,768]{1,0:T(8,128)(2,1)S(1)} %get-tuple-element.100.gated_ref, bf16[768,768]{1,0:T(8,128)(2,1)S(1)} %get-tuple-element.101.wout_ref), custom_call_target="tpu_custom_call" | custom-call | flops 1000000000 | bytes 49152 | tf_op jit(solution)/shard_map/pallas_call | solution.py:63
  33.8 3.0 %collective-permute-done.10.odd_ref = bf16[16,128]{1,0:T(8,128)(2,1)S(1)} collective-permute-done((bf16[16,128]{1,0:T(8,128)(2,1)S(1)}, bf16[16,128]{1,0:T(8,128)(2,1)S(1)}, u32[]{:S(2)}, u32[]{:S(2)}) %collective-permute-start.10) | collective-permute-done | bytes 4128 | tf_op jit(solution)/shard_map/ppermute | solution.py:472
  36.8 1.1 %shard_map.206 = f32[3,384]{1,0:T(4,128)} custom-call(f32[1,384]{1,0:T(1,128)S(1)} %get-tuple-element.68.living_ref, bf16[384,64]{1,0:T(8,128)(2,1)S(1)} %get-tuple-element.69.hot_ref, f32[384,128]{1,0:T(8,128)S(1)} %get-tuple-element.70.mid_ref, bf16[32,128]{1,0:T(8,128)(2,1)S(1)} %get-tuple-element.97.back_ref, ...), custom_call_target="tpu_custom_call" | custom-call | flops 10000000 | bytes 4608 | tf_op jit(solution)/shard_map/pallas_call | solution.py:63
  (24 shorter events, 0.5 us)
Async XLA Ops:
  3.4 3.1 %collective-permute-start = (bf16[96,128]{1,0:T(8,128)(2,1)S(1)}, bf16[96,128]{1,0:T(8,128)(2,1)S(1)}, u32[]{:S(2)}, u32[]{:S(2)}) collective-permute-start(bf16[96,128]{1,0:T(8,128)(2,1)S(1)} %get-tuple-element.63), channel_id=1, source_target_pairs={{0,1},{1,0},{2,3},{3,2},{4,5},{5,4},{6,7},{7,6},{8,9},{9,8},{10,11... | collective-permute-start | bytes 73736 | tf_op jit(solution)/shard_map/ppermute | solution.py:473
  3.5 4.2 %collective-permute-start.1 = (bf16[96,128]{1,0:T(8,128)(2,1)S(1)}, bf16[96,128]{1,0:T(8,128)(2,1)S(1)}, u32[]{:S(2)}, u32[]{:S(2)}) collective-permute-start(bf16[96,128]{1,0:T(8,128)(2,1)S(1)} %get-tuple-element.64), channel_id=1, source_target_pairs={{1,2},{3,4},{5,6},{7,8},{9,10},{11,12},{13,14},{2,1},{4,3},{6,5},{... | collective-permute-start | bytes 73736 | tf_op jit(solution)/shard_map/ppermute | solution.py:472
  9.6 4.4 %collective-permute-start.2 = (bf16[16,896]{1,0:T(8,128)(2,1)S(1)}, bf16[16,896]{1,0:T(8,128)(2,1)S(1)}, u32[]{:S(2)}, u32[]{:S(2)}) collective-permute-start(bf16[16,896]{1,0:T(8,128)(2,1)S(1)} %get-tuple-element.72), channel_id=1, source_target_pairs={{0,1},{1,0},{2,3},{3,2},{4,5},{5,4},{6,7},{7,6},{8,9},{9,8},{10,11... | collective-permute-start | bytes 86024 | tf_op jit(solution)/shard_map/ppermute | solution.py:473
  9.7 4.3 %collective-permute-start.3 = (bf16[16,896]{1,0:T(8,128)(2,1)S(1)}, bf16[16,896]{1,0:T(8,128)(2,1)S(1)}, u32[]{:S(2)}, u32[]{:S(2)}) collective-permute-start(bf16[16,896]{1,0:T(8,128)(2,1)S(1)} %get-tuple-element.73), channel_id=1, source_target_pairs={{1,2},{3,4},{5,6},{7,8},{9,10},{11,12},{13,14},{2,1},{4,3},{6,5},{... | collective-permute-start | bytes 86024 | tf_op jit(solution)/shard_map/ppermute | solution.py:472
  11.2 2.8 %copy-start.1 = (bf16[32,768]{1,0:T(8,128)(2,1)S(1)}, bf16[32,768]{1,0:T(8,128)(2,1)}, u32[]{:S(2)}) copy-start(bf16[32,768]{1,0:T(8,128)(2,1)} %single_ref.1) | copy-start | bytes 147460
  11.2 3.2 %copy-start = (bf16[768,2304]{1,0:T(8,128)(2,1)S(1)}, bf16[768,2304]{1,0:T(8,128)(2,1)}, u32[]{:S(2)}) copy-start(bf16[768,2304]{1,0:T(8,128)(2,1)} %wqkv_ref.9) | copy-start | bytes 10616836
  14.3 5.9 %collective-permute-start.4 = (bf16[32,768]{1,0:T(8,128)(2,1)S(1)}, bf16[32,768]{1,0:T(8,128)(2,1)S(1)}, u32[]{:S(2)}, u32[]{:S(2)}) collective-permute-start(bf16[32,768]{1,0:T(8,128)(2,1)S(1)} %get-tuple-element.77.norm_ref), channel_id=1, source_target_pairs={{0,9},{1,8},{2,11},{3,10},{4,13},{5,12},{6,15},{7,14},{8,1},{9,0},... | collective-permute-start | bytes 147464 | tf_op jit(solution)/shard_map/ppermute | solution.py:496
  20.2 4.1 %collective-permute-start.5 = (bf16[64,768]{1,0:T(8,128)(2,1)S(1)}, bf16[64,768]{1,0:T(8,128)(2,1)S(1)}, u32[]{:S(2)}, u32[]{:S(2)}) collective-permute-start(bf16[64,768]{1,0:T(8,128)(2,1)S(1)} %get-tuple-element.104.after), channel_id=1, source_target_pairs={{0,5},{1,2},{2,1},{3,6},{4,7},{5,0},{6,3},{7,4},{8,13},{9,10},{10,... | collective-permute-start | bytes 294920 | tf_op jit(solution)/shard_map/ppermute | solution.py:496
  24.4 1.5 %collective-permute-start.7 = (bf16[128,768]{1,0:T(8,128)(2,1)S(1)}, bf16[128,768]{1,0:T(8,128)(2,1)S(1)}, u32[]{:S(2)}, u32[]{:S(2)}) collective-permute-start(bf16[128,768]{1,0:T(8,128)(2,1)S(1)} %constant_dynamic-update-slice_fusion.2.keys_ref), channel_id=1, source_target_pairs={{0,1},{1,0},{2,3},{3,2},{4,5},{5,4},{6,7},{7,6},{8,9},{9,8},{10,11... | collective-permute-start | bytes 589832 | tf_op jit(solution)/shard_map/ppermute | solution.py:496
  24.5 5.1 %collective-permute-start.6 = (bf16[128,768]{1,0:T(8,128)(2,1)S(1)}, bf16[128,768]{1,0:T(8,128)(2,1)S(1)}, u32[]{:S(2)}, u32[]{:S(2)}) collective-permute-start(bf16[128,768]{1,0:T(8,128)(2,1)S(1)} %constant_dynamic-update-slice_fusion.2.keys_ref), channel_id=1, source_target_pairs={{0,3},{1,4},{2,7},{3,0},{4,1},{5,6},{6,5},{7,2},{8,11},{9,12},{10,... | collective-permute-start | bytes 589832 | tf_op jit(solution)/shard_map/ppermute | solution.py:496
  29.6 1.5 %collective-permute-start.8 = (bf16[128,768]{1,0:T(8,128)(2,1)S(1)}, bf16[128,768]{1,0:T(8,128)(2,1)S(1)}, u32[]{:S(2)}, u32[]{:S(2)}) collective-permute-start(bf16[128,768]{1,0:T(8,128)(2,1)S(1)} %collective-permute-done.6.keys_ref), channel_id=1, source_target_pairs={{0,1},{1,0},{2,3},{3,2},{4,5},{5,4},{6,7},{7,6},{8,9},{9,8},{10,11... | collective-permute-start | bytes 589832 | tf_op jit(solution)/shard_map/ppermute | solution.py:496
  32.5 4.3 %collective-permute-start.9 = (bf16[16,128]{1,0:T(8,128)(2,1)S(1)}, bf16[16,128]{1,0:T(8,128)(2,1)S(1)}, u32[]{:S(2)}, u32[]{:S(2)}) collective-permute-start(bf16[16,128]{1,0:T(8,128)(2,1)S(1)} %get-tuple-element.98), channel_id=1, source_target_pairs={{0,1},{1,0},{2,3},{3,2},{4,5},{5,4},{6,7},{7,6},{8,9},{9,8},{10,11... | collective-permute-start | bytes 12296 | tf_op jit(solution)/shard_map/ppermute | solution.py:473
  32.8 3.9 %collective-permute-start.10 = (bf16[16,128]{1,0:T(8,128)(2,1)S(1)}, bf16[16,128]{1,0:T(8,128)(2,1)S(1)}, u32[]{:S(2)}, u32[]{:S(2)}) collective-permute-start(bf16[16,128]{1,0:T(8,128)(2,1)S(1)} %get-tuple-element.99), channel_id=1, source_target_pairs={{1,2},{3,4},{5,6},{7,8},{9,10},{11,12},{13,14},{2,1},{4,3},{6,5},{... | collective-permute-start | bytes 12296 | tf_op jit(solution)/shard_map/ppermute | solution.py:472
  32.8 3.9 %copy-start.2 = (f32[3,384]{1,0:T(4,128)S(1)}, f32[3,384]{1,0:T(4,128)}, u32[]{:S(2)}) copy-start(f32[3,384]{1,0:T(4,128)} %pos_ref.1) | copy-start | bytes 13828
  32.8 3.9 %copy-start.3 = (f32[3,384]{1,0:T(4,128)S(1)}, f32[3,384]{1,0:T(4,128)}, u32[]{:S(2)}) copy-start(f32[3,384]{1,0:T(4,128)} %noise_ref.1) | copy-start | bytes 13828
  32.8 3.9 %copy-start.4 = (bf16[3,128]{1,0:T(4,128)(2,1)S(1)}, bf16[3,128]{1,0:T(4,128)(2,1)}, u32[]{:S(2)}) copy-start(bf16[3,128]{1,0:T(4,128)(2,1)} %wpos_ref.1) | copy-start | bytes 2308
where the time goes:
time: 38.1 us; the launch traced here: 37.9 us
  Pallas kernels  17.1 us (45%)
  waiting for transfers between devices  15 us (39%)
  starting transfers between devices  4.22 us (11%)
  between operations  1.44 us (4%)
    pallas_call x13, Pallas kernels, call(): run(*[pltpu.with_memory_space_constraint(x, pltpu.HBM) if h and x.size >...  17.1 us
    ppermute x5, waiting for transfers between devices, swap(): lax.ppermute(value, 'row', [(i, i ^ step[kind_of(i)]) for i in range(coun...  9.5 us
    ppermute x3, waiting for transfers between devices, exchange(): odd = lax.ppermute(odd, ('grp', 'row'), far)  5.52 us
    ppermute x3, starting transfers between devices, exchange(): odd = lax.ppermute(odd, ('grp', 'row'), far)  3.01 us
  transfers between devices with their start and end apart: 11, of which 7 were waited for; matrix products, arithmetic and copies ran while one was open for 0% of the time, Pallas kernels for 27%

commit v1 on v0

--- a/solution.py
+++ b/solution.py
@@ -300,18 +300,39 @@
         copy.wait()
 
 
-def query_body(norm_ref, wqkv_ref, query_ref):
-    rows, model = norm_ref.shape
-    width = model // TH
-    group = TH // 2
-    span = group * width
-    own = iota((group * rows, span), 0) // rows == iota((group * rows, span), 1) // width
-    tq = dot(norm_ref[...], wqkv_ref[:, :model])
-    for g in range(2):
-        part = tq[:, g * span : (g + 1) * span]
-        stacked = jnp.where(own, jnp.concatenate([part] * group, axis=0), 0.0).astype(BF16)
-        wk = wqkv_ref[:, model + g * span : model + (g + 1) * span]
-        query_ref[g * group * rows : (g + 1) * group * rows, :] = dot_nt(stacked, wk).astype(BF16)
+def query_body(
+    norm_ref,
+    in_ref,
+    wqkv_ref,
+    wout_hbm,
+    wback_hbm,
+    query_ref,
+    wout_ref,
+    both_ref,
+    base_ref,
+    wback_ref,
+    sems,
+):
+    copies = fetch(sems, (wback_hbm, wback_ref), *quarters(wout_hbm, wout_ref))
+
+    @pl.when(lax.axis_index("row") >= 0)
+    def _():
+        rows, model = norm_ref.shape
+        width = model // TH
+        group = TH // 2
+        span = group * width
+        own = iota((group * rows, span), 0) // rows == iota((group * rows, span), 1) // width
+        tq = dot(norm_ref[...], wqkv_ref[:, :model])
+        for g in range(2):
+            part = tq[:, g * span : (g + 1) * span]
+            stacked = jnp.where(own, jnp.concatenate([part] * group, axis=0), 0.0).astype(BF16)
+            wk = wqkv_ref[:, model + g * span : model + (g + 1) * span]
+            query_ref[g * group * rows : (g + 1) * group * rows, :] = dot_nt(stacked, wk).astype(BF16)
+
+    for copy in copies:
+        copy.wait()
+    both_ref[...] = dot(wout_ref[...], wback_ref[...]).astype(BF16)
+    base_ref[...] = dot(in_ref[...].astype(BF16), wback_ref[...])
 
 
 def stage_body(lists, after, norm_ref, bias_ref, mask_ref, wgate_hbm, out_ref, gate_ref, wgate_ref, sems):
@@ -346,18 +367,6 @@
     gate_ref[...] = jax.nn.sigmoid(dot(norm_ref[...], wgate_ref[...]))
 
 
-def weights_of(copies, in_ref, wout_ref, wback_ref, both_ref, base_ref):
-    for copy in copies:
-        copy.wait()
-    both_ref[...] = dot(wout_ref[...], wback_ref[...]).astype(BF16)
-    base_ref[...] = dot(in_ref[...].astype(BF16), wback_ref[...])
-
-
-def weights_body(in_ref, wout_hbm, wback_hbm, wout_ref, both_ref, base_ref, wback_ref, sems):
-    copies = fetch(sems, (wback_hbm, wback_ref), *quarters(wout_hbm, wout_ref))
-    weights_of(copies, in_ref, wout_ref, wback_ref, both_ref, base_ref)
-
-
 def part_of(rows, query_ref, keys_ref, bias, wqkv_ref):
     model = query_ref.shape[1]
     width = model // TH
@@ -389,31 +398,6 @@
     found = part_of(part_ref.shape[1], query_ref, keys_ref, lambda at: bias_ref[chunk, at, :], wqkv_ref)
     for n in range(3):
         part_ref[n] = found[n]
-
-
-def second_body(
-    chunk,
-    query_ref,
-    keys_ref,
-    bias_ref,
-    wqkv_ref,
-    in_ref,
-    wout_hbm,
-    wback_hbm,
-    part_ref,
-    wout_ref,
-    both_ref,
-    base_ref,
-    wback_ref,
-    sems,
-):
-    copies = fetch(sems, (wback_hbm, wback_ref), *quarters(wout_hbm, wout_ref))
-
-    @pl.when(lax.axis_index("row") >= 0)
-    def _():
-        part_body(chunk, query_ref, keys_ref, bias_ref, wqkv_ref, part_ref)
-
-    weights_of(copies, in_ref, wout_ref, wback_ref, both_ref, base_ref)
 
 
 def attend_body(
@@ -608,8 +592,17 @@
 
     def query(seen):
         return call(
-            query_body, [shape((TH * block_rows, model), BF16)], [VMEM] * 2, flops=10**9
-        )(seen, w_tok_qkv)[0]
+            query_body,
+            [
+                shape((TH * block_rows, model), BF16),
+                shape(w_tok_out.shape, BF16),
+                shape(w_back.shape, BF16),
+                shape((block_rows, width), F32),
+            ],
+            [VMEM] * 3 + [HBM] * 2,
+            [pltpu.VMEM(w_back.shape, BF16), pltpu.SemaphoreType.DMA((5,))],
+            flops=10**9,
+        )(seen, token_in, w_tok_qkv, w_tok_out, w_back)
 
     def stage(seen):
         return call(
@@ -620,18 +613,6 @@
             flops=10**9,
         )(seen, norm, raw, mask, w_tok_gate)
 
-    made = [shape(w_tok_out.shape, BF16), shape(w_back.shape, BF16), shape((block_rows, width), F32)]
-    kept = [pltpu.VMEM(w_back.shape, BF16), pltpu.SemaphoreType.DMA((5,))]
-
-    def second(chunk, seen):
-        return call(
-            functools.partial(second_body, chunk),
-            [shape((3, block_rows, model), F32)] + made,
-            [VMEM] * 5 + [HBM] * 2,
-            kept,
-            flops=10**9,
-        )(query_rows, seen, score_bias, w_tok_qkv, token_in, w_tok_out, w_back)
-
     def part(chunk, seen):
         return call(
             functools.partial(part_body, chunk),
@@ -645,22 +626,20 @@
         for n, step in enumerate(steps[:-1]):
             arrived = swap(held, count, step)
             if n == 0:
-                arrived, query_rows = lax.optimization_barrier((arrived, query(norm)))
+                arrived, (query_rows, wout, both, base) = lax.optimization_barrier((arrived, query(norm)))
             if n == 1:
                 arrived, (score_bias, gate) = lax.optimization_barrier((arrived, stage(held)))
             held = jnp.concatenate([held, arrived], axis=0)
         last = swap(held, count, steps[-1])
         near = swap(held, count, [1, 1])
-        after, wout, both, base = second(1, near)
-        parts = [part(0, held), after]
-        last, parts, wout, both, base = lax.optimization_barrier((last, parts, wout, both, base))
+        parts = [part(0, held), part(1, near)]
+        last, parts = lax.optimization_barrier((last, parts))
         end = swap(last, count, [1, 1])
         parts = parts + [part(2, last)]
     else:
         end = lax.all_gather(norm, "row", axis=0, tiled=True)
-        query_rows = query(norm)
+        query_rows, wout, both, base = query(norm)
         score_bias, gate = stage(norm)
-        wout, both, base = call(weights_body, made, [VMEM] + [HBM] * 2, kept)(token_in, w_tok_out, w_back)
         parts = []
     gated, back, pair, odd = call(
         functools.partial(attend_body, half, chunks - 1),

time: 38.1 us -> 38.1 us (level)
  transfers between devices with their start and end apart: 11 -> 11, of which waited for: 7 -> 7; matrix products, arithmetic and copies ran while one was open for 0% -> 0% of each run, Pallas kernels for 27% -> 28%
where the time goes in v1:
time: 38.1 us; the launch traced here: 37.9 us
  Pallas kernels  17.4 us (46%)
  waiting for transfers between devices  14.7 us (39%)
  starting transfers between devices  4.23 us (11%)
  between operations  1.44 us (4%)
    pallas_call x13, Pallas kernels, call(): run(*[pltpu.with_memory_space_constraint(x, pltpu.HBM) if h and x.size >...  17.4 us
    ppermute x5, waiting for transfers between devices, swap(): lax.ppermute(value, 'row', [(i, i ^ step[kind_of(i)]) for i in range(coun...  9.21 us
    ppermute x3, waiting for transfers between devices, exchange(): odd = lax.ppermute(odd, ('grp', 'row'), far)  5.51 us
    ppermute x3, starting transfers between devices, exchange(): odd = lax.ppermute(odd, ('grp', 'row'), far)  3.02 us
  transfers between devices with their start and end apart: 11, of which 7 were waited for; matrix products, arithmetic and copies ran while one was open for 0% of the time, Pallas kernels for 28%

profile of v1, /device:TPU:24, one launch (start us, length us, event | category | flops | bytes accessed | tf_op | source)
XLA Modules:
  0.0 37.9 jit_solution(15770981548599813665)
XLA Ops:
  1.3 2.1 %shard_map.194 = (s32[8]{0:T(128)S(1)}, f32[384,128]{1,0:T(8,128)S(1)}, bf16[384,128]{1,0:T(8,128)(2,1)S(1)}, bf16[96,128]{1,0:T(8,128)(2,1)S(1)}, bf16[96,128]{...) custom-call(s32[1,1]{1,0:T(1,128)} %bitcast.2.counts_hbm, ...), custom_call_target="tpu_custom_call" | custom-call | flops 10000000 | bytes 1459792 | tf_op jit(solution)/shard_map/pallas_call | solution.py:63
  3.5 1.5 %collective-permute-start.1 = (bf16[96,128]{1,0:T(8,128)(2,1)S(1)}, bf16[96,128]{1,0:T(8,128)(2,1)S(1)}, u32[]{:S(2)}, u32[]{:S(2)}) collective-permute-start(bf16[96,128]{1,0:T(8,128)(2,1)S(1)} %get-tuple-element.64), channel_id=1, source_target_pairs={{1,2},{3,4},{5,6},{7,8},{9,10},{11,12},{13,14},{2,1},{4,3},{6,5},{... | collective-permute-start | bytes 73736 | tf_op jit(solution)/shard_map/ppermute | solution.py:456
  5.0 1.5 %shard_map.195 = (bf16[384,128]{1,0:T(8,128)(2,1)S(1)}, f32[480,128]{1,0:T(8,128)S(1)}, f32[480,128]{1,0:T(8,128)S(1)}, bf16[384,128]{1,0:T(8,128)(2,1)S(1)}) custom-call(s32[1,12]{1,0:T(1,128)S(1)} %get-tuple-element.54.offsets, bf16[384,128]{1,0:T(8,128)(2,1)S(1)} %get-tuple-element.57.normed_ref, bf16[128,384]{1,0:T(8,128)(2,1)S(1)} %get-tuple-element.58.wqkv_ref, ...), custom_call_target="tpu_custom_call" | custom-call | flops 1000000000 | bytes 688128 | tf_op jit(solution)/shard_map/pallas_call | solution.py:63
  6.5 1.2 %collective-permute-done.1.odd_ref = bf16[96,128]{1,0:T(8,128)(2,1)S(1)} collective-permute-done((bf16[96,128]{1,0:T(8,128)(2,1)S(1)}, bf16[96,128]{1,0:T(8,128)(2,1)S(1)}, u32[]{:S(2)}, u32[]{:S(2)}) %collective-permute-start.1) | collective-permute-done | bytes 24608 | tf_op jit(solution)/shard_map/ppermute | solution.py:456
  7.7 1.8 %shard_map.196 = (f32[384,128]{1,0:T(8,128)S(1)}, f32[32,896]{1,0:T(8,128)S(1)}, bf16[16,896]{1,0:T(8,128)(2,1)S(1)}, bf16[16,896]{1,0:T(8,128)(2,1)S(1)}, bf16[...) custom-call(s32[8]{0:T(128)S(1)} %get-tuple-element.53.info, s32[1,12]{1,0:T(1,128)S(1)} %get-tuple-element.54.offsets, ...), custom_call_target="tpu_custom_call" | custom-call | flops 10000000 | bytes 419328 | tf_op jit(solution)/shard_map/pallas_call | solution.py:63
  9.7 1.5 %collective-permute-start.3 = (bf16[16,896]{1,0:T(8,128)(2,1)S(1)}, bf16[16,896]{1,0:T(8,128)(2,1)S(1)}, u32[]{:S(2)}, u32[]{:S(2)}) collective-permute-start(bf16[16,896]{1,0:T(8,128)(2,1)S(1)} %get-tuple-element.73), channel_id=1, source_target_pairs={{1,2},{3,4},{5,6},{7,8},{9,10},{11,12},{13,14},{2,1},{4,3},{6,5},{... | collective-permute-start | bytes 86024 | tf_op jit(solution)/shard_map/ppermute | solution.py:456
  11.2 1.4 %shard_map.197 = (f32[16,32,512]{2,1,0:T(8,128)S(1)}, s32[32,512]{1,0:T(8,128)S(1)}) custom-call(f32[32,896]{1,0:T(8,128)S(1)} %get-tuple-element.71.after.own_ref, f32[16,32,512]{2,1,0:T(8,128)} %bias_hbm.3, s32[32,512]{1,0:T(8,128)} %mask_hbm.1), custom_call_target="tpu_custom_call" | custom-call | flops 1000000000 | bytes 1114112 | tf_op jit(solution)/shard_map/pallas_call | solution.py:63
  12.6 1.3 %collective-permute-done.3.odd_ref = bf16[16,896]{1,0:T(8,128)(2,1)S(1)} collective-permute-done((bf16[16,896]{1,0:T(8,128)(2,1)S(1)}, bf16[16,896]{1,0:T(8,128)(2,1)S(1)}, u32[]{:S(2)}, u32[]{:S(2)}) %collective-permute-start.3) | collective-permute-done | bytes 28704 | tf_op jit(solution)/shard_map/ppermute | solution.py:456
  13.9 0.3 shard_map.198
  14.4 1.9 %shard_map.199 = (bf16[512,768]{1,0:T(8,128)(2,1)S(1)}, bf16[768,768]{1,0:T(8,128)(2,1)S(1)}, bf16[768,128]{1,0:T(8,128)(2,1)S(1)}, f32[32,128]{1,0:T(8,128)S(1)}) custom-call(bf16[32,768]{1,0:T(8,128)(2,1)S(1)} %get-tuple-element.77.norm_ref, f32[32,768]{1,0:T(8,128)S(1)} %get-tuple-element.78.in_ref, bf16[768,2304]{1,0:T(8,128)(2,1)S(1)} %copy-done, ...), custom_call_target="tpu_custom_call" | custom-call | flops 1000000000 | bytes 2179072 | tf_op jit(solution)/shard_map/pallas_call | solution.py:63
  16.3 4.0 %collective-permute-done.4 = bf16[32,768]{1,0:T(8,128)(2,1)S(1)} collective-permute-done((bf16[32,768]{1,0:T(8,128)(2,1)S(1)}, bf16[32,768]{1,0:T(8,128)(2,1)S(1)}, u32[]{:S(2)}, u32[]{:S(2)}) %collective-permute-start.4) | collective-permute-done | bytes 49184 | tf_op jit(solution)/shard_map/ppermute | solution.py:480
  20.3 1.6 %shard_map.200 = (f32[4,512,128]{2,1,0:T(8,128)S(1)}, f32[32,768]{1,0:T(8,128)S(1)}) custom-call(bf16[64,768]{1,0:T(8,128)(2,1)S(1)} %get-tuple-element.105.after, bf16[32,768]{1,0:T(8,128)(2,1)S(1)} %get-tuple-element.77.norm_ref, f32[16,32,512]{2,1,0:T(8,128)S(1)} %get-tuple-element.86.bias_ref, s32[32,512]{1,0:T(8,128)S(1)} %get-tuple-element.87.mask_ref, ...), custom_call_target="tpu_custom_call" | custom-call | flops 1000000000 | bytes 1146880 | tf_op jit(solution)/shard_map/pallas_call | solution.py:63
  21.9 2.4 %collective-permute-done.5 = bf16[64,768]{1,0:T(8,128)(2,1)S(1)} collective-permute-done((bf16[64,768]{1,0:T(8,128)(2,1)S(1)}, bf16[64,768]{1,0:T(8,128)(2,1)S(1)}, u32[]{:S(2)}, u32[]{:S(2)}) %collective-permute-start.5) | collective-permute-done | bytes 98336 | tf_op jit(solution)/shard_map/ppermute | solution.py:480
  24.5 1.1 %shard_map.201.rest_0_ = f32[3,32,768]{2,1,0:T(8,128)S(1)} custom-call(bf16[512,768]{1,0:T(8,128)(2,1)S(1)} %get-tuple-element.84.query_ref, bf16[128,768]{1,0:T(8,128)(2,1)S(1)} %constant_dynamic-update-slice_fusion.2.keys_ref, f32[4,512,128]{2,1,0:T(8,128)S(1)} %get-tuple-element.92.bias_ref, bf16[768,2304]{1,0:T(8,128)(2,1)S(1)} %copy-done), custom_call_target="tpu_custom_call" | custom-call | flops 1000000000 | bytes 294912 | tf_op jit(solution)/shard_map/pallas_call | solution.py:63
  25.7 0.2 collective-permute-done.7.keys_ref
  25.9 1.1 %shard_map.202.rest_1_ = f32[3,32,768]{2,1,0:T(8,128)S(1)} custom-call(bf16[512,768]{1,0:T(8,128)(2,1)S(1)} %get-tuple-element.84.query_ref, bf16[128,768]{1,0:T(8,128)(2,1)S(1)} %collective-permute-done.7.keys_ref, f32[4,512,128]{2,1,0:T(8,128)S(1)} %get-tuple-element.92.bias_ref, bf16[768,2304]{1,0:T(8,128)(2,1)S(1)} %copy-done), custom_call_target="tpu_custom_call" | custom-call | flops 1000000000 | bytes 294912 | tf_op jit(solution)/shard_map/pallas_call | solution.py:63
  27.0 2.6 %collective-permute-done.6.keys_ref = bf16[128,768]{1,0:T(8,128)(2,1)S(1)} collective-permute-done((bf16[128,768]{1,0:T(8,128)(2,1)S(1)}, bf16[128,768]{1,0:T(8,128)(2,1)S(1)}, u32[]{:S(2)}, u32[]{:S(2)}) %collective-permute-start.6) | collective-permute-done | bytes 196640 | tf_op jit(solution)/shard_map/ppermute | solution.py:480
  29.6 0.4 %collective-permute-start.8 = (bf16[128,768]{1,0:T(8,128)(2,1)S(1)}, bf16[128,768]{1,0:T(8,128)(2,1)S(1)}, u32[]{:S(2)}, u32[]{:S(2)}) collective-permute-start(bf16[128,768]{1,0:T(8,128)(2,1)S(1)} %collective-permute-done.6.keys_ref), channel_id=1, source_target_pairs={{0,1},{1,0},{2,3},{3,2},{4,5},{5,4},{6,7},{7,6},{8,9},{9,8},{10,11... | collective-permute-start | bytes 589832 | tf_op jit(solution)/shard_map/ppermute | solution.py:480
  30.0 1.1 %shard_map.203.rest_2_ = f32[3,32,768]{2,1,0:T(8,128)S(1)} custom-call(bf16[512,768]{1,0:T(8,128)(2,1)S(1)} %get-tuple-element.84.query_ref, bf16[128,768]{1,0:T(8,128)(2,1)S(1)} %collective-permute-done.6.keys_ref, f32[4,512,128]{2,1,0:T(8,128)S(1)} %get-tuple-element.92.bias_ref, bf16[768,2304]{1,0:T(8,128)(2,1)S(1)} %copy-done), custom_call_target="tpu_custom_call" | custom-call | flops 1000000000 | bytes 294912 | tf_op jit(solution)/shard_map/pallas_call | solution.py:63
  31.2 1.3 %shard_map.204 = (bf16[32,768]{1,0:T(8,128)(2,1)S(1)}, bf16[32,128]{1,0:T(8,128)(2,1)S(1)}, bf16[16,128]{1,0:T(8,128)(2,1)S(1)}, bf16[16,128]{1,0:T(8,128)(2,1)S(1)}) custom-call(f32[32,128]{1,0:T(8,128)S(1)} %get-tuple-element.83.base_ref, bf16[512,768]{1,0:T(8,128)(2,1)S(1)} %get-tuple-element.84.query_ref, f32[32,768]{1,0:T(8,128)S(1)} %get-tuple-element.90.gate_ref, ...), custom_call_target="tpu_custom_call" | custom-call | flops 10000000 | bytes 65536 | tf_op jit(solution)/shard_map/pallas_call | solution.py:63
  32.5 0.3 collective-permute-start.9
  32.9 1.0 %shard_map.205 = bf16[32,768]{1,0:T(8,128)(2,1)} custom-call(f32[32,768]{1,0:T(8,128)S(1)} %get-tuple-element.78.in_ref, bf16[32,768]{1,0:T(8,128)(2,1)S(1)} %get-tuple-element.100.gated_ref, bf16[768,768]{1,0:T(8,128)(2,1)S(1)} %get-tuple-element.101.wout_ref), custom_call_target="tpu_custom_call" | custom-call | flops 1000000000 | bytes 49152 | tf_op jit(solution)/shard_map/pallas_call | solution.py:63
  33.8 3.0 %collective-permute-done.10.odd_ref = bf16[16,128]{1,0:T(8,128)(2,1)S(1)} collective-permute-done((bf16[16,128]{1,0:T(8,128)(2,1)S(1)}, bf16[16,128]{1,0:T(8,128)(2,1)S(1)}, u32[]{:S(2)}, u32[]{:S(2)}) %collective-permute-start.10) | collective-permute-done | bytes 4128 | tf_op jit(solution)/shard_map/ppermute | solution.py:456
  36.8 1.1 %shard_map.206 = f32[3,384]{1,0:T(4,128)} custom-call(f32[1,384]{1,0:T(1,128)S(1)} %get-tuple-element.68.living_ref, bf16[384,64]{1,0:T(8,128)(2,1)S(1)} %get-tuple-element.69.hot_ref, f32[384,128]{1,0:T(8,128)S(1)} %get-tuple-element.70.mid_ref, bf16[32,128]{1,0:T(8,128)(2,1)S(1)} %get-tuple-element.97.back_ref, ...), custom_call_target="tpu_custom_call" | custom-call | flops 10000000 | bytes 4608 | tf_op jit(solution)/shard_map/pallas_call | solution.py:63
  (24 shorter events, 0.5 us)
Async XLA Ops:
  3.4 3.1 %collective-permute-start = (bf16[96,128]{1,0:T(8,128)(2,1)S(1)}, bf16[96,128]{1,0:T(8,128)(2,1)S(1)}, u32[]{:S(2)}, u32[]{:S(2)}) collective-permute-start(bf16[96,128]{1,0:T(8,128)(2,1)S(1)} %get-tuple-element.63), channel_id=1, source_target_pairs={{0,1},{1,0},{2,3},{3,2},{4,5},{5,4},{6,7},{7,6},{8,9},{9,8},{10,11... | collective-permute-start | bytes 73736 | tf_op jit(solution)/shard_map/ppermute | solution.py:457
  3.5 4.2 %collective-permute-start.1 = (bf16[96,128]{1,0:T(8,128)(2,1)S(1)}, bf16[96,128]{1,0:T(8,128)(2,1)S(1)}, u32[]{:S(2)}, u32[]{:S(2)}) collective-permute-start(bf16[96,128]{1,0:T(8,128)(2,1)S(1)} %get-tuple-element.64), channel_id=1, source_target_pairs={{1,2},{3,4},{5,6},{7,8},{9,10},{11,12},{13,14},{2,1},{4,3},{6,5},{... | collective-permute-start | bytes 73736 | tf_op jit(solution)/shard_map/ppermute | solution.py:456
  9.6 4.4 %collective-permute-start.2 = (bf16[16,896]{1,0:T(8,128)(2,1)S(1)}, bf16[16,896]{1,0:T(8,128)(2,1)S(1)}, u32[]{:S(2)}, u32[]{:S(2)}) collective-permute-start(bf16[16,896]{1,0:T(8,128)(2,1)S(1)} %get-tuple-element.72), channel_id=1, source_target_pairs={{0,1},{1,0},{2,3},{3,2},{4,5},{5,4},{6,7},{7,6},{8,9},{9,8},{10,11... | collective-permute-start | bytes 86024 | tf_op jit(solution)/shard_map/ppermute | solution.py:457
  9.7 4.3 %collective-permute-start.3 = (bf16[16,896]{1,0:T(8,128)(2,1)S(1)}, bf16[16,896]{1,0:T(8,128)(2,1)S(1)}, u32[]{:S(2)}, u32[]{:S(2)}) collective-permute-start(bf16[16,896]{1,0:T(8,128)(2,1)S(1)} %get-tuple-element.73), channel_id=1, source_target_pairs={{1,2},{3,4},{5,6},{7,8},{9,10},{11,12},{13,14},{2,1},{4,3},{6,5},{... | collective-permute-start | bytes 86024 | tf_op jit(solution)/shard_map/ppermute | solution.py:456
  11.2 2.8 %copy-start.1 = (bf16[32,768]{1,0:T(8,128)(2,1)S(1)}, bf16[32,768]{1,0:T(8,128)(2,1)}, u32[]{:S(2)}) copy-start(bf16[32,768]{1,0:T(8,128)(2,1)} %single_ref.1) | copy-start | bytes 147460
  11.2 3.2 %copy-start = (bf16[768,2304]{1,0:T(8,128)(2,1)S(1)}, bf16[768,2304]{1,0:T(8,128)(2,1)}, u32[]{:S(2)}) copy-start(bf16[768,2304]{1,0:T(8,128)(2,1)} %wqkv_ref.9) | copy-start | bytes 10616836
  14.3 6.0 %collective-permute-start.4 = (bf16[32,768]{1,0:T(8,128)(2,1)S(1)}, bf16[32,768]{1,0:T(8,128)(2,1)S(1)}, u32[]{:S(2)}, u32[]{:S(2)}) collective-permute-start(bf16[32,768]{1,0:T(8,128)(2,1)S(1)} %get-tuple-element.77.norm_ref), channel_id=1, source_target_pairs={{0,9},{1,8},{2,11},{3,10},{4,13},{5,12},{6,15},{7,14},{8,1},{9,0},... | collective-permute-start | bytes 147464 | tf_op jit(solution)/shard_map/ppermute | solution.py:480
  20.2 4.1 %collective-permute-start.5 = (bf16[64,768]{1,0:T(8,128)(2,1)S(1)}, bf16[64,768]{1,0:T(8,128)(2,1)S(1)}, u32[]{:S(2)}, u32[]{:S(2)}) collective-permute-start(bf16[64,768]{1,0:T(8,128)(2,1)S(1)} %get-tuple-element.105.after), channel_id=1, source_target_pairs={{0,5},{1,2},{2,1},{3,6},{4,7},{5,0},{6,3},{7,4},{8,13},{9,10},{10,... | collective-permute-start | bytes 294920 | tf_op jit(solution)/shard_map/ppermute | solution.py:480
  24.4 1.5 %collective-permute-start.7 = (bf16[128,768]{1,0:T(8,128)(2,1)S(1)}, bf16[128,768]{1,0:T(8,128)(2,1)S(1)}, u32[]{:S(2)}, u32[]{:S(2)}) collective-permute-start(bf16[128,768]{1,0:T(8,128)(2,1)S(1)} %constant_dynamic-update-slice_fusion.2.keys_ref), channel_id=1, source_target_pairs={{0,1},{1,0},{2,3},{3,2},{4,5},{5,4},{6,7},{7,6},{8,9},{9,8},{10,11... | collective-permute-start | bytes 589832 | tf_op jit(solution)/shard_map/ppermute | solution.py:480
  24.5 5.1 %collective-permute-start.6 = (bf16[128,768]{1,0:T(8,128)(2,1)S(1)}, bf16[128,768]{1,0:T(8,128)(2,1)S(1)}, u32[]{:S(2)}, u32[]{:S(2)}) collective-permute-start(bf16[128,768]{1,0:T(8,128)(2,1)S(1)} %constant_dynamic-update-slice_fusion.2.keys_ref), channel_id=1, source_target_pairs={{0,3},{1,4},{2,7},{3,0},{4,1},{5,6},{6,5},{7,2},{8,11},{9,12},{10,... | collective-permute-start | bytes 589832 | tf_op jit(solution)/shard_map/ppermute | solution.py:480
  29.6 1.5 %collective-permute-start.8 = (bf16[128,768]{1,0:T(8,128)(2,1)S(1)}, bf16[128,768]{1,0:T(8,128)(2,1)S(1)}, u32[]{:S(2)}, u32[]{:S(2)}) collective-permute-start(bf16[128,768]{1,0:T(8,128)(2,1)S(1)} %collective-permute-done.6.keys_ref), channel_id=1, source_target_pairs={{0,1},{1,0},{2,3},{3,2},{4,5},{5,4},{6,7},{7,6},{8,9},{9,8},{10,11... | collective-permute-start | bytes 589832 | tf_op jit(solution)/shard_map/ppermute | solution.py:480
  32.5 4.3 %collective-permute-start.9 = (bf16[16,128]{1,0:T(8,128)(2,1)S(1)}, bf16[16,128]{1,0:T(8,128)(2,1)S(1)}, u32[]{:S(2)}, u32[]{:S(2)}) collective-permute-start(bf16[16,128]{1,0:T(8,128)(2,1)S(1)} %get-tuple-element.98), channel_id=1, source_target_pairs={{0,1},{1,0},{2,3},{3,2},{4,5},{5,4},{6,7},{7,6},{8,9},{9,8},{10,11... | collective-permute-start | bytes 12296 | tf_op jit(solution)/shard_map/ppermute | solution.py:457
  32.8 3.9 %collective-permute-start.10 = (bf16[16,128]{1,0:T(8,128)(2,1)S(1)}, bf16[16,128]{1,0:T(8,128)(2,1)S(1)}, u32[]{:S(2)}, u32[]{:S(2)}) collective-permute-start(bf16[16,128]{1,0:T(8,128)(2,1)S(1)} %get-tuple-element.99), channel_id=1, source_target_pairs={{1,2},{3,4},{5,6},{7,8},{9,10},{11,12},{13,14},{2,1},{4,3},{6,5},{... | collective-permute-start | bytes 12296 | tf_op jit(solution)/shard_map/ppermute | solution.py:456
  32.8 3.9 %copy-start.2 = (f32[3,384]{1,0:T(4,128)S(1)}, f32[3,384]{1,0:T(4,128)}, u32[]{:S(2)}) copy-start(f32[3,384]{1,0:T(4,128)} %pos_ref.1) | copy-start | bytes 13828
  32.8 3.9 %copy-start.3 = (f32[3,384]{1,0:T(4,128)S(1)}, f32[3,384]{1,0:T(4,128)}, u32[]{:S(2)}) copy-start(f32[3,384]{1,0:T(4,128)} %noise_ref.1) | copy-start | bytes 13828
  32.8 3.9 %copy-start.4 = (bf16[3,128]{1,0:T(4,128)(2,1)S(1)}, bf16[3,128]{1,0:T(4,128)(2,1)}, u32[]{:S(2)}) copy-start(bf16[3,128]{1,0:T(4,128)(2,1)} %wpos_ref.1) | copy-start | bytes 2308

commit v2 on v1

--- a/solution.py
+++ b/solution.py
@@ -459,14 +459,16 @@
 
 
 def kind_of(i):
-    return (i ^ (i >> 1) ^ (i >> 2)) & 1
+    for shift in (16, 8, 4, 2, 1):
+        i = i ^ (i >> shift)
+    return i & 1
 
 
 def gather_plan(count):
     bits = [1 << b for b in range(count.bit_length() - 1, 0, -1) if 1 << b < count]
     steps = [[b | 1, b | 1] for b in bits]
-    high, low = bits[-2] | 1, bits[-1] | 1
-    steps[-2:] = [[high, low], [low, high]]
+    top, high, low = (b | 1 for b in bits[-3:])
+    steps[-3:] = [[high, top], [top, low], [low, high]]
     lists = [[0], [0]]
     for step in steps[:-1]:
         lists = [lists[p] + [x ^ step[p] for x in lists[p ^ kind_of(step[p])]] for p in range(2)]

time: 38.1 us -> 38.3 us (level)
  the two profiles are of different devices: /device:TPU:24 before, /device:TPU:0 now
where the time goes in v2:
time: 38.3 us; the launch traced here: 38.1 us
  Pallas kernels  17.4 us (45%)
  starting transfers between devices  15.3 us (40%)
  waiting for transfers between devices  3.86 us (10%)
  between operations  1.41 us (4%)
    pallas_call x13, Pallas kernels, call(): run(*[pltpu.with_memory_space_constraint(x, pltpu.HBM) if h and x.size >...  17.4 us
    ppermute x5, starting transfers between devices, swap(): lax.ppermute(value, 'row', [(i, i ^ step[kind_of(i)]) for i in range(coun...  8.23 us
    ppermute x3, starting transfers between devices, exchange(): odd = lax.ppermute(odd, ('grp', 'row'), far)  6.07 us
    ppermute x5, waiting for transfers between devices, swap(): lax.ppermute(value, 'row', [(i, i ^ step[kind_of(i)]) for i in range(coun...  1.97 us
    ppermute x3, waiting for transfers between devices, exchange(): odd = lax.ppermute(odd, ('grp', 'row'), far)  1.89 us
    ppermute x3, starting transfers between devices, exchange(): pair = lax.ppermute(pair, 'row', near)  1.02 us
  transfers between devices with their start and end apart: 11, of which 6 were waited for; matrix products, arithmetic and copies ran while one was open for 0% of the time, Pallas kernels for 28%

profile of v2, /device:TPU:0, one launch (start us, length us, event | category | flops | bytes accessed | tf_op | source)
XLA Modules:
  0.0 38.1 jit_solution(5679274743772544879)
XLA Ops:
  1.3 2.1 %shard_map.194 = (s32[8]{0:T(128)S(1)}, f32[384,128]{1,0:T(8,128)S(1)}, bf16[384,128]{1,0:T(8,128)(2,1)S(1)}, bf16[96,128]{1,0:T(8,128)(2,1)S(1)}, bf16[96,128]{...) custom-call(s32[1,1]{1,0:T(1,128)} %bitcast.2.counts_hbm, ...), custom_call_target="tpu_custom_call" | custom-call | flops 10000000 | bytes 1459792 | tf_op jit(solution)/shard_map/pallas_call | solution.py:63
  3.4 0.6 %collective-permute-start = (bf16[96,128]{1,0:T(8,128)(2,1)S(1)}, bf16[96,128]{1,0:T(8,128)(2,1)S(1)}, u32[]{:S(2)}, u32[]{:S(2)}) collective-permute-start(bf16[96,128]{1,0:T(8,128)(2,1)S(1)} %get-tuple-element.63), channel_id=1, source_target_pairs={{0,1},{1,0},{2,3},{3,2},{4,5},{5,4},{6,7},{7,6},{8,9},{9,8},{10,11... | collective-permute-start | bytes 73736 | tf_op jit(solution)/shard_map/ppermute | solution.py:457
  4.0 2.6 %collective-permute-start.1 = (bf16[96,128]{1,0:T(8,128)(2,1)S(1)}, bf16[96,128]{1,0:T(8,128)(2,1)S(1)}, u32[]{:S(2)}, u32[]{:S(2)}) collective-permute-start(bf16[96,128]{1,0:T(8,128)(2,1)S(1)} %get-tuple-element.64), channel_id=1, source_target_pairs={{1,2},{3,4},{5,6},{7,8},{9,10},{11,12},{13,14},{2,1},{4,3},{6,5},{... | collective-permute-start | bytes 73736 | tf_op jit(solution)/shard_map/ppermute | solution.py:456
  6.5 1.5 %shard_map.195 = (bf16[384,128]{1,0:T(8,128)(2,1)S(1)}, f32[480,128]{1,0:T(8,128)S(1)}, f32[480,128]{1,0:T(8,128)S(1)}, bf16[384,128]{1,0:T(8,128)(2,1)S(1)}) custom-call(s32[1,12]{1,0:T(1,128)S(1)} %get-tuple-element.54.offsets, bf16[384,128]{1,0:T(8,128)(2,1)S(1)} %get-tuple-element.57.normed_ref, bf16[128,384]{1,0:T(8,128)(2,1)S(1)} %get-tuple-element.58.wqkv_ref, ...), custom_call_target="tpu_custom_call" | custom-call | flops 1000000000 | bytes 688128 | tf_op jit(solution)/shard_map/pallas_call | solution.py:63
  8.3 1.8 %shard_map.196 = (f32[384,128]{1,0:T(8,128)S(1)}, f32[32,896]{1,0:T(8,128)S(1)}, bf16[16,896]{1,0:T(8,128)(2,1)S(1)}, bf16[16,896]{1,0:T(8,128)(2,1)S(1)}, bf16[...) custom-call(s32[8]{0:T(128)S(1)} %get-tuple-element.53.info, s32[1,12]{1,0:T(1,128)S(1)} %get-tuple-element.54.offsets, ...), custom_call_target="tpu_custom_call" | custom-call | flops 10000000 | bytes 419328 | tf_op jit(solution)/shard_map/pallas_call | solution.py:63
  10.4 2.0 %collective-permute-start.3 = (bf16[16,896]{1,0:T(8,128)(2,1)S(1)}, bf16[16,896]{1,0:T(8,128)(2,1)S(1)}, u32[]{:S(2)}, u32[]{:S(2)}) collective-permute-start(bf16[16,896]{1,0:T(8,128)(2,1)S(1)} %get-tuple-element.73), channel_id=1, source_target_pairs={{1,2},{3,4},{5,6},{7,8},{9,10},{11,12},{13,14},{2,1},{4,3},{6,5},{... | collective-permute-start | bytes 86024 | tf_op jit(solution)/shard_map/ppermute | solution.py:456
  12.4 1.4 %shard_map.197 = (f32[16,32,512]{2,1,0:T(8,128)S(1)}, s32[32,512]{1,0:T(8,128)S(1)}) custom-call(f32[32,896]{1,0:T(8,128)S(1)} %get-tuple-element.71.after.own_ref, f32[16,32,512]{2,1,0:T(8,128)} %bias_hbm.3, s32[32,512]{1,0:T(8,128)} %mask_hbm.1), custom_call_target="tpu_custom_call" | custom-call | flops 1000000000 | bytes 1114112 | tf_op jit(solution)/shard_map/pallas_call | solution.py:63
  13.8 0.4 %collective-permute-done.3.odd_ref = bf16[16,896]{1,0:T(8,128)(2,1)S(1)} collective-permute-done((bf16[16,896]{1,0:T(8,128)(2,1)S(1)}, bf16[16,896]{1,0:T(8,128)(2,1)S(1)}, u32[]{:S(2)}, u32[]{:S(2)}) %collective-permute-start.3) | collective-permute-done | bytes 28704 | tf_op jit(solution)/shard_map/ppermute | solution.py:456
  14.3 0.3 shard_map.198
  14.6 2.2 %collective-permute-start.4 = (bf16[32,768]{1,0:T(8,128)(2,1)S(1)}, bf16[32,768]{1,0:T(8,128)(2,1)S(1)}, u32[]{:S(2)}, u32[]{:S(2)}) collective-permute-start(bf16[32,768]{1,0:T(8,128)(2,1)S(1)} %get-tuple-element.77.norm_ref), channel_id=1, source_target_pairs={{0,5},{1,8},{2,11},{3,6},{4,13},{5,0},{6,3},{7,14},{8,1},{9,12},{1... | collective-permute-start | bytes 147464 | tf_op jit(solution)/shard_map/ppermute | solution.py:482
  16.8 1.9 %shard_map.199 = (bf16[512,768]{1,0:T(8,128)(2,1)S(1)}, bf16[768,768]{1,0:T(8,128)(2,1)S(1)}, bf16[768,128]{1,0:T(8,128)(2,1)S(1)}, f32[32,128]{1,0:T(8,128)S(1)}) custom-call(bf16[32,768]{1,0:T(8,128)(2,1)S(1)} %get-tuple-element.77.norm_ref, f32[32,768]{1,0:T(8,128)S(1)} %get-tuple-element.78.in_ref, bf16[768,2304]{1,0:T(8,128)(2,1)S(1)} %copy-done, ...), custom_call_target="tpu_custom_call" | custom-call | flops 1000000000 | bytes 2179072 | tf_op jit(solution)/shard_map/pallas_call | solution.py:63
  18.8 3.4 %collective-permute-start.5 = (bf16[64,768]{1,0:T(8,128)(2,1)S(1)}, bf16[64,768]{1,0:T(8,128)(2,1)S(1)}, u32[]{:S(2)}, u32[]{:S(2)}) collective-permute-start(bf16[64,768]{1,0:T(8,128)(2,1)S(1)} %get-tuple-element.105.after), channel_id=1, source_target_pairs={{0,9},{1,2},{2,1},{3,10},{4,7},{5,12},{6,15},{7,4},{8,11},{9,0},{1... | collective-permute-start | bytes 294920 | tf_op jit(solution)/shard_map/ppermute | solution.py:482
  22.1 1.6 %shard_map.200 = (f32[4,512,128]{2,1,0:T(8,128)S(1)}, f32[32,768]{1,0:T(8,128)S(1)}) custom-call(bf16[64,768]{1,0:T(8,128)(2,1)S(1)} %get-tuple-element.105.after, bf16[32,768]{1,0:T(8,128)(2,1)S(1)} %get-tuple-element.77.norm_ref, f32[16,32,512]{2,1,0:T(8,128)S(1)} %get-tuple-element.86.bias_ref, s32[32,512]{1,0:T(8,128)S(1)} %get-tuple-element.87.mask_ref, ...), custom_call_target="tpu_custom_call" | custom-call | flops 1000000000 | bytes 1146880 | tf_op jit(solution)/shard_map/pallas_call | solution.py:63
  23.8 0.7 %collective-permute-done.5 = bf16[64,768]{1,0:T(8,128)(2,1)S(1)} collective-permute-done((bf16[64,768]{1,0:T(8,128)(2,1)S(1)}, bf16[64,768]{1,0:T(8,128)(2,1)S(1)}, u32[]{:S(2)}, u32[]{:S(2)}) %collective-permute-start.5) | collective-permute-done | bytes 98336 | tf_op jit(solution)/shard_map/ppermute | solution.py:482
  24.6 2.3 %collective-permute-start.6 = (bf16[128,768]{1,0:T(8,128)(2,1)S(1)}, bf16[128,768]{1,0:T(8,128)(2,1)S(1)}, u32[]{:S(2)}, u32[]{:S(2)}) collective-permute-start(bf16[128,768]{1,0:T(8,128)(2,1)S(1)} %constant_dynamic-update-slice_fusion.2.keys_ref), channel_id=1, source_target_pairs={{0,3},{1,4},{2,7},{3,0},{4,1},{5,6},{6,5},{7,2},{8,13},{9,10},{10,... | collective-permute-start | bytes 589832 | tf_op jit(solution)/shard_map/ppermute | solution.py:482
  27.0 1.1 %shard_map.201.rest_0_ = f32[3,32,768]{2,1,0:T(8,128)S(1)} custom-call(bf16[512,768]{1,0:T(8,128)(2,1)S(1)} %get-tuple-element.84.query_ref, bf16[128,768]{1,0:T(8,128)(2,1)S(1)} %constant_dynamic-update-slice_fusion.2.keys_ref, f32[4,512,128]{2,1,0:T(8,128)S(1)} %get-tuple-element.92.bias_ref, bf16[768,2304]{1,0:T(8,128)(2,1)S(1)} %copy-done), custom_call_target="tpu_custom_call" | custom-call | flops 1000000000 | bytes 294912 | tf_op jit(solution)/shard_map/pallas_call | solution.py:63
  28.1 1.1 %shard_map.202.rest_1_ = f32[3,32,768]{2,1,0:T(8,128)S(1)} custom-call(bf16[512,768]{1,0:T(8,128)(2,1)S(1)} %get-tuple-element.84.query_ref, bf16[128,768]{1,0:T(8,128)(2,1)S(1)} %collective-permute-done.7.keys_ref, f32[4,512,128]{2,1,0:T(8,128)S(1)} %get-tuple-element.92.bias_ref, bf16[768,2304]{1,0:T(8,128)(2,1)S(1)} %copy-done), custom_call_target="tpu_custom_call" | custom-call | flops 1000000000 | bytes 294912 | tf_op jit(solution)/shard_map/pallas_call | solution.py:63
  29.2 1.1 %collective-permute-done.6.keys_ref = bf16[128,768]{1,0:T(8,128)(2,1)S(1)} collective-permute-done((bf16[128,768]{1,0:T(8,128)(2,1)S(1)}, bf16[128,768]{1,0:T(8,128)(2,1)S(1)}, u32[]{:S(2)}, u32[]{:S(2)}) %collective-permute-start.6) | collective-permute-done | bytes 196640 | tf_op jit(solution)/shard_map/ppermute | solution.py:482
  30.4 1.1 %shard_map.203.rest_2_ = f32[3,32,768]{2,1,0:T(8,128)S(1)} custom-call(bf16[512,768]{1,0:T(8,128)(2,1)S(1)} %get-tuple-element.84.query_ref, bf16[128,768]{1,0:T(8,128)(2,1)S(1)} %collective-permute-done.6.keys_ref, f32[4,512,128]{2,1,0:T(8,128)S(1)} %get-tuple-element.92.bias_ref, bf16[768,2304]{1,0:T(8,128)(2,1)S(1)} %copy-done), custom_call_target="tpu_custom_call" | custom-call | flops 1000000000 | bytes 294912 | tf_op jit(solution)/shard_map/pallas_call | solution.py:63
  31.8 1.3 %shard_map.204 = (bf16[32,768]{1,0:T(8,128)(2,1)S(1)}, bf16[32,128]{1,0:T(8,128)(2,1)S(1)}, bf16[16,128]{1,0:T(8,128)(2,1)S(1)}, bf16[16,128]{1,0:T(8,128)(2,1)S(1)}) custom-call(f32[32,128]{1,0:T(8,128)S(1)} %get-tuple-element.83.base_ref, bf16[512,768]{1,0:T(8,128)(2,1)S(1)} %get-tuple-element.84.query_ref, f32[32,768]{1,0:T(8,128)S(1)} %get-tuple-element.90.gate_ref, ...), custom_call_target="tpu_custom_call" | custom-call | flops 10000000 | bytes 65536 | tf_op jit(solution)/shard_map/pallas_call | solution.py:63
  33.3 1.5 %collective-permute-start.10 = (bf16[16,128]{1,0:T(8,128)(2,1)S(1)}, bf16[16,128]{1,0:T(8,128)(2,1)S(1)}, u32[]{:S(2)}, u32[]{:S(2)}) collective-permute-start(bf16[16,128]{1,0:T(8,128)(2,1)S(1)} %get-tuple-element.99), channel_id=1, source_target_pairs={{1,2},{3,4},{5,6},{7,8},{9,10},{11,12},{13,14},{2,1},{4,3},{6,5},{... | collective-permute-start | bytes 12296 | tf_op jit(solution)/shard_map/ppermute | solution.py:456
  34.8 0.9 %shard_map.205 = bf16[32,768]{1,0:T(8,128)(2,1)} custom-call(f32[32,768]{1,0:T(8,128)S(1)} %get-tuple-element.78.in_ref, bf16[32,768]{1,0:T(8,128)(2,1)S(1)} %get-tuple-element.100.gated_ref, bf16[768,768]{1,0:T(8,128)(2,1)S(1)} %get-tuple-element.101.wout_ref), custom_call_target="tpu_custom_call" | custom-call | flops 1000000000 | bytes 49152 | tf_op jit(solution)/shard_map/pallas_call | solution.py:63
  35.8 1.2 %collective-permute-done.10.odd_ref = bf16[16,128]{1,0:T(8,128)(2,1)S(1)} collective-permute-done((bf16[16,128]{1,0:T(8,128)(2,1)S(1)}, bf16[16,128]{1,0:T(8,128)(2,1)S(1)}, u32[]{:S(2)}, u32[]{:S(2)}) %collective-permute-start.10) | collective-permute-done | bytes 4128 | tf_op jit(solution)/shard_map/ppermute | solution.py:456
  37.0 1.1 %shard_map.206 = f32[3,384]{1,0:T(4,128)} custom-call(f32[1,384]{1,0:T(1,128)S(1)} %get-tuple-element.68.living_ref, bf16[384,64]{1,0:T(8,128)(2,1)S(1)} %get-tuple-element.69.hot_ref, f32[384,128]{1,0:T(8,128)S(1)} %get-tuple-element.70.mid_ref, bf16[32,128]{1,0:T(8,128)(2,1)S(1)} %get-tuple-element.97.back_ref, ...), custom_call_target="tpu_custom_call" | custom-call | flops 10000000 | bytes 4608 | tf_op jit(solution)/shard_map/pallas_call | solution.py:63
  (24 shorter events, 1.3 us)
Async XLA Ops:
  3.4 4.6 %collective-permute-start = (bf16[96,128]{1,0:T(8,128)(2,1)S(1)}, bf16[96,128]{1,0:T(8,128)(2,1)S(1)}, u32[]{:S(2)}, u32[]{:S(2)}) collective-permute-start(bf16[96,128]{1,0:T(8,128)(2,1)S(1)} %get-tuple-element.63), channel_id=1, source_target_pairs={{0,1},{1,0},{2,3},{3,2},{4,5},{5,4},{6,7},{7,6},{8,9},{9,8},{10,11... | collective-permute-start | bytes 73736 | tf_op jit(solution)/shard_map/ppermute | solution.py:457
  4.0 4.4 %collective-permute-start.1 = (bf16[96,128]{1,0:T(8,128)(2,1)S(1)}, bf16[96,128]{1,0:T(8,128)(2,1)S(1)}, u32[]{:S(2)}, u32[]{:S(2)}) collective-permute-start(bf16[96,128]{1,0:T(8,128)(2,1)S(1)} %get-tuple-element.64), channel_id=1, source_target_pairs={{1,2},{3,4},{5,6},{7,8},{9,10},{11,12},{13,14},{2,1},{4,3},{6,5},{... | collective-permute-start | bytes 73736 | tf_op jit(solution)/shard_map/ppermute | solution.py:456
  10.2 4.1 %collective-permute-start.2 = (bf16[16,896]{1,0:T(8,128)(2,1)S(1)}, bf16[16,896]{1,0:T(8,128)(2,1)S(1)}, u32[]{:S(2)}, u32[]{:S(2)}) collective-permute-start(bf16[16,896]{1,0:T(8,128)(2,1)S(1)} %get-tuple-element.72), channel_id=1, source_target_pairs={{0,1},{1,0},{2,3},{3,2},{4,5},{5,4},{6,7},{7,6},{8,9},{9,8},{10,11... | collective-permute-start | bytes 86024 | tf_op jit(solution)/shard_map/ppermute | solution.py:457
  10.4 3.9 %collective-permute-start.3 = (bf16[16,896]{1,0:T(8,128)(2,1)S(1)}, bf16[16,896]{1,0:T(8,128)(2,1)S(1)}, u32[]{:S(2)}, u32[]{:S(2)}) collective-permute-start(bf16[16,896]{1,0:T(8,128)(2,1)S(1)} %get-tuple-element.73), channel_id=1, source_target_pairs={{1,2},{3,4},{5,6},{7,8},{9,10},{11,12},{13,14},{2,1},{4,3},{6,5},{... | collective-permute-start | bytes 86024 | tf_op jit(solution)/shard_map/ppermute | solution.py:456
  12.4 1.9 %copy-start.1 = (bf16[32,768]{1,0:T(8,128)(2,1)S(1)}, bf16[32,768]{1,0:T(8,128)(2,1)}, u32[]{:S(2)}) copy-start(bf16[32,768]{1,0:T(8,128)(2,1)} %single_ref.1) | copy-start | bytes 147460
  12.4 4.4 %copy-start = (bf16[768,2304]{1,0:T(8,128)(2,1)S(1)}, bf16[768,2304]{1,0:T(8,128)(2,1)}, u32[]{:S(2)}) copy-start(bf16[768,2304]{1,0:T(8,128)(2,1)} %wqkv_ref.9) | copy-start | bytes 10616836
  14.6 4.1 %collective-permute-start.4 = (bf16[32,768]{1,0:T(8,128)(2,1)S(1)}, bf16[32,768]{1,0:T(8,128)(2,1)S(1)}, u32[]{:S(2)}, u32[]{:S(2)}) collective-permute-start(bf16[32,768]{1,0:T(8,128)(2,1)S(1)} %get-tuple-element.77.norm_ref), channel_id=1, source_target_pairs={{0,5},{1,8},{2,11},{3,6},{4,13},{5,0},{6,3},{7,14},{8,1},{9,12},{1... | collective-permute-start | bytes 147464 | tf_op jit(solution)/shard_map/ppermute | solution.py:482
  18.8 5.7 %collective-permute-start.5 = (bf16[64,768]{1,0:T(8,128)(2,1)S(1)}, bf16[64,768]{1,0:T(8,128)(2,1)S(1)}, u32[]{:S(2)}, u32[]{:S(2)}) collective-permute-start(bf16[64,768]{1,0:T(8,128)(2,1)S(1)} %get-tuple-element.105.after), channel_id=1, source_target_pairs={{0,9},{1,2},{2,1},{3,10},{4,7},{5,12},{6,15},{7,4},{8,11},{9,0},{1... | collective-permute-start | bytes 294920 | tf_op jit(solution)/shard_map/ppermute | solution.py:482
  24.5 3.6 %collective-permute-start.7 = (bf16[128,768]{1,0:T(8,128)(2,1)S(1)}, bf16[128,768]{1,0:T(8,128)(2,1)S(1)}, u32[]{:S(2)}, u32[]{:S(2)}) collective-permute-start(bf16[128,768]{1,0:T(8,128)(2,1)S(1)} %constant_dynamic-update-slice_fusion.2.keys_ref), channel_id=1, source_target_pairs={{0,1},{1,0},{2,3},{3,2},{4,5},{5,4},{6,7},{7,6},{8,9},{9,8},{10,11... | collective-permute-start | bytes 589832 | tf_op jit(solution)/shard_map/ppermute | solution.py:482
  24.6 5.7 %collective-permute-start.6 = (bf16[128,768]{1,0:T(8,128)(2,1)S(1)}, bf16[128,768]{1,0:T(8,128)(2,1)S(1)}, u32[]{:S(2)}, u32[]{:S(2)}) collective-permute-start(bf16[128,768]{1,0:T(8,128)(2,1)S(1)} %constant_dynamic-update-slice_fusion.2.keys_ref), channel_id=1, source_target_pairs={{0,3},{1,4},{2,7},{3,0},{4,1},{5,6},{6,5},{7,2},{8,13},{9,10},{10,... | collective-permute-start | bytes 589832 | tf_op jit(solution)/shard_map/ppermute | solution.py:482
  30.3 1.4 %collective-permute-start.8 = (bf16[128,768]{1,0:T(8,128)(2,1)S(1)}, bf16[128,768]{1,0:T(8,128)(2,1)S(1)}, u32[]{:S(2)}, u32[]{:S(2)}) collective-permute-start(bf16[128,768]{1,0:T(8,128)(2,1)S(1)} %collective-permute-done.6.keys_ref), channel_id=1, source_target_pairs={{0,1},{1,0},{2,3},{3,2},{4,5},{5,4},{6,7},{7,6},{8,9},{9,8},{10,11... | collective-permute-start | bytes 589832 | tf_op jit(solution)/shard_map/ppermute | solution.py:482
  33.1 3.9 %collective-permute-start.9 = (bf16[16,128]{1,0:T(8,128)(2,1)S(1)}, bf16[16,128]{1,0:T(8,128)(2,1)S(1)}, u32[]{:S(2)}, u32[]{:S(2)}) collective-permute-start(bf16[16,128]{1,0:T(8,128)(2,1)S(1)} %get-tuple-element.98), channel_id=1, source_target_pairs={{0,1},{1,0},{2,3},{3,2},{4,5},{5,4},{6,7},{7,6},{8,9},{9,8},{10,11... | collective-permute-start | bytes 12296 | tf_op jit(solution)/shard_map/ppermute | solution.py:457
  33.3 3.6 %collective-permute-start.10 = (bf16[16,128]{1,0:T(8,128)(2,1)S(1)}, bf16[16,128]{1,0:T(8,128)(2,1)S(1)}, u32[]{:S(2)}, u32[]{:S(2)}) collective-permute-start(bf16[16,128]{1,0:T(8,128)(2,1)S(1)} %get-tuple-element.99), channel_id=1, source_target_pairs={{1,2},{3,4},{5,6},{7,8},{9,10},{11,12},{13,14},{2,1},{4,3},{6,5},{... | collective-permute-start | bytes 12296 | tf_op jit(solution)/shard_map/ppermute | solution.py:456
  34.8 2.1 %copy-start.2 = (f32[3,384]{1,0:T(4,128)S(1)}, f32[3,384]{1,0:T(4,128)}, u32[]{:S(2)}) copy-start(f32[3,384]{1,0:T(4,128)} %pos_ref.1) | copy-start | bytes 13828
  34.8 2.1 %copy-start.3 = (f32[3,384]{1,0:T(4,128)S(1)}, f32[3,384]{1,0:T(4,128)}, u32[]{:S(2)}) copy-start(f32[3,384]{1,0:T(4,128)} %noise_ref.1) | copy-start | bytes 13828
  34.8 2.1 %copy-start.4 = (bf16[3,128]{1,0:T(4,128)(2,1)S(1)}, bf16[3,128]{1,0:T(4,128)(2,1)}, u32[]{:S(2)}) copy-start(bf16[3,128]{1,0:T(4,128)(2,1)} %wpos_ref.1) | copy-start | bytes 2308
